TPU v7x, 512 devices: a whole 4x8x8 slice. The times are simulated.
512 devices in a mesh: row: 16 (over x_hi, y), col: 8 (over z), depth: 4 (over x_lo, core).
Axes of the slice: x: 4 (x_hi: 2, x_lo: 2; x = x_hi * 2 + x_lo), y: 8, z: 8, core: 2. Of those that a mesh axis runs over, the one named last changes fastest.
Arguments:
- x_vals: bfloat16 [16, 64, 4, 128, 128], P('row', ('col', 'depth')), may hold values from -2.5 to 2.5
- x_rows: int32 [16, 64, 4], P('row', ('col', 'depth')), may hold values from -1 to 3, as said below
- out_block: int32 [16, 8, 4], P('row', 'col', 'depth'), may hold values from 0 to 15, as said below
Outputs:
- product_blocks: bfloat16 [16, 8, 4, 128, 128], P('row', 'col', 'depth')
Inputs may be any that keep to these rules, and one draw needn't show every extreme that they name: `x_rows`: within one row group and block column the filled slots name distinct rows. In every row group, each run of 2 block columns that starts at a multiple of 2 has a column with all 4 slots filled. `out_block`: within one tile the 4 entries are distinct positions, and every tile lists position 15 among them.
All inputs are finite; a program needn't handle non-finite values.
Results may differ from a plain program's by a relative error of at most 0.001.
Values may be sent and summed in bfloat16 or wider, within the bound.
No kernel may reach another device: no remote copies, remote signals or barrier semaphores. Data moves between devices by JAX's collectives and lax.ppermute only.
A program may use at most 128 MiB of HBM per device.

v0:
```python
import jax
import jax.numpy as jnp
from jax import lax
from jax.sharding import PartitionSpec as P


def shifted(value, axis, steps):
    count = lax.axis_size(axis)
    pairs = [(source, (source + steps) % count) for source in range(count)]
    return lax.ppermute(value, axis, pairs)


def accumulate(partial_value, operands, positions, group_rows):
    left_vals, left_rows, right_vals, right_rows = operands
    slot_total = left_vals.shape[0] * left_vals.shape[1]
    left_valid = left_rows >= 0
    for slot_index in range(right_vals.shape[1]):
        partner_slot = right_vals[:, slot_index]
        right_slot_rows = right_rows[:, slot_index]
        blocks = jnp.einsum(
            "ksab,kcb->ksac", left_vals, partner_slot, preferred_element_type=jnp.float32
        )
        target = left_rows * group_rows + right_slot_rows[:, None]
        target = jnp.where(left_valid & (right_slot_rows >= 0)[:, None], target, -1)
        select = (target.reshape(1, slot_total) == positions[:, None]).astype(jnp.float32)
        gained = jnp.dot(
            select,
            blocks.reshape(slot_total, -1),
            precision=lax.Precision.HIGHEST,
            preferred_element_type=jnp.float32,
        )
        partial_value = partial_value + gained.reshape(partial_value.shape)
    return partial_value


def on_device(x_vals, x_rows, out_block):
    row_count = lax.axis_size("row")
    col_count = lax.axis_size("col")
    depth_count = lax.axis_size("depth")
    col_index = lax.axis_index("col")
    midpoint = col_count // 2
    group_rows = x_vals.shape[1] * col_count * depth_count // row_count
    positions = lax.all_gather(out_block, "depth", axis=2, tiled=True).reshape(-1)
    home_vals = x_vals[0]
    home_rows = x_rows[0]
    partial_value = jnp.zeros((positions.shape[0],) + x_vals.shape[3:], jnp.float32)
    up_count = jnp.maximum(midpoint - col_index, 0)
    down_count = jnp.maximum(col_index - midpoint, 0)
    partner_vals, partner_rows = (home_vals, home_rows)
    for round_number in range(midpoint):
        arrived = shifted((partner_vals, partner_rows), "row", 1)
        use_moved = round_number < up_count
        partner_vals = jnp.where(use_moved, arrived[0], partner_vals)
        partner_rows = jnp.where(use_moved, arrived[1], partner_rows)
    for round_number in range(col_count - 1 - midpoint):
        arrived = shifted((partner_vals, partner_rows), "row", -1)
        use_moved = round_number < down_count
        partner_vals = jnp.where(use_moved, arrived[0], partner_vals)
        partner_rows = jnp.where(use_moved, arrived[1], partner_rows)
    operands = (home_vals, home_rows, partner_vals, partner_rows)
    partial_value = accumulate(partial_value, operands, positions, group_rows)
    at_first = col_index == 0
    current = operands
    for round_number in range(1, col_count):
        arrived = shifted((current[2], current[3]), "row", 1)
        wrapped = shifted((current[2], current[3]), "row", 1 - col_count)
        moved_vals = jnp.where(at_first, wrapped[0], arrived[0])
        moved_rows = jnp.where(at_first, wrapped[1], arrived[1])
        current = shifted((current[0], current[1], moved_vals, moved_rows), "col", -1)
        partial_value = accumulate(partial_value, current, positions, group_rows)
    summed = lax.psum_scatter(partial_value, "depth", scatter_dimension=0, tiled=True)
    return summed.astype(jnp.bfloat16).reshape(out_block.shape + x_vals.shape[3:])


def solution(mesh):
    in_specs = (
        P("row", ("col", "depth"), None, None, None),
        P("row", ("col", "depth"), None),
        P("row", "col", "depth"),
    )
    out_specs = P("row", "col", "depth", None, None)
    return jax.shard_map(
        on_device, mesh=mesh, in_specs=in_specs, out_specs=out_specs, check_vma=False
    )
```

profile of v0, /device:TPU:1, one launch (start us, length us, event | category | flops | bytes accessed | tf_op | source)
XLA Modules:
  0.0 485.6 jit_solution(7261423711008481838)
XLA Ops:
  7.5 4.2 collective-permute-start.7
  11.7 10.7 %collective-permute-start.21 = (bf16[2,4,128,128]{3,2,0,1:T(8,128)(2,1)S(1)}, bf16[2,4,128,128]{3,2,0,1:T(8,128)(2,1)S(1)}, u32[]{:S(2)}, u32[]{:S(2)}) collective-permute-start(bf16[2,4,128,128]{3,2,0,1:T(8,128)(2,1)S(1)} %bitcast.729), channel_id=1, source_target_pairs={{0,28},{4,0},{8,4},{12,8},{16,12},{20,16},{24,20},{28,24},{1,29},{... | collective-permute-start | bytes 786440 | tf_op jit(solution)/shard_map/ppermute | solution.py:10
  30.6 5.3 %all-reduce = s32[4]{0:T(128)S(1)} all-reduce(s32[4]{0:T(128)S(1)} %bitcast_dynamic-update-slice_fusion), channel_id=1, replica_groups=mesh['row'=16,'col'=8,'depth'=4] {'depth'}, use_global_device_ids=true, to_apply=%add | all-reduce | flops 4 | bytes 32
  65.2 5.7 %collective-permute-start.5 = (s32[2,4]{1,0:T(2,128)S(1)}, s32[2,4]{1,0:T(2,128)S(1)}, u32[]{:S(2)}, u32[]{:S(2)}) collective-permute-start(s32[2,4]{1,0:T(2,128)S(1)} %broadcast_select_fusion.25), channel_id=1, source_target_pairs={{0,480},{32,0},{64,32},{96,64},{128,96},{160,128},{192,160},{224,1... | collective-permute-start | bytes 104 | tf_op jit(solution)/shard_map/ppermute | solution.py:10
  73.1 5.7 %collective-permute-start.6 = (s32[2,4]{1,0:T(2,128)S(1)}, s32[2,4]{1,0:T(2,128)S(1)}, u32[]{:S(2)}, u32[]{:S(2)}) collective-permute-start(s32[2,4]{1,0:T(2,128)S(1)} %broadcast_select_fusion.26), channel_id=1, source_target_pairs={{0,480},{32,0},{64,32},{96,64},{128,96},{160,128},{192,160},{224,1... | collective-permute-start | bytes 104 | tf_op jit(solution)/shard_map/ppermute | solution.py:10
  102.3 4.3 collective-permute-done.24
  117.3 4.3 collective-permute-done.32
  137.1 4.8 collective-permute-start.41
  153.3 4.8 collective-permute-start.49
  159.0 4.8 collective-permute-start.29
  172.9 4.7 collective-permute-done.9
  188.4 6.3 %collective-permute-start.11 = (bf16[2,4,128,128]{3,2,0,1:T(8,128)(2,1)S(1)}, bf16[2,4,128,128]{3,2,0,1:T(8,128)(2,1)S(1)}, u32[]{:S(2)}, u32[]{:S(2)}) collective-permute-start(bf16[2,4,128,128]{3,2,0,1:T(8,128)(2,1)S(1)} %broadcast_select_fusion.10), channel_id=1, source_target_pairs={{0,480},{32,0},{64,32},{96,64},{128,96},{160,128},{192,160},{224,1... | collective-permute-start | bytes 786440 | tf_op jit(solution)/shard_map/ppermute | solution.py:10
  201.5 6.6 %collective-permute-start.12 = (bf16[2,4,128,128]{3,2,0,1:T(8,128)(2,1)S(1)}, bf16[2,4,128,128]{3,2,0,1:T(8,128)(2,1)S(1)}, u32[]{:S(2)}, u32[]{:S(2)}) collective-permute-start(bf16[2,4,128,128]{3,2,0,1:T(8,128)(2,1)S(1)} %broadcast_select_fusion.11), channel_id=1, source_target_pairs={{0,480},{32,0},{64,32},{96,64},{128,96},{160,128},{192,160},{224,1... | collective-permute-start | bytes 786440 | tf_op jit(solution)/shard_map/ppermute | solution.py:10
  208.2 4.6 collective-permute-start.65
  213.7 4.8 collective-permute-start.61
  222.3 4.8 collective-permute-start.69
  250.5 4.2 collective-permute-done.20
  268.9 4.6 collective-permute-done.27
  273.5 4.5 collective-permute-start.28
  287.1 4.6 collective-permute-start.35
  295.4 6.2 %collective-permute-done.35 = bf16[2,4,128,128]{3,2,0,1:T(8,128)(2,1)} collective-permute-done((bf16[2,4,128,128]{3,2,0,1:T(8,128)(2,1)}, bf16[2,4,128,128]{3,2,0,1:T(8,128)(2,1)}, u32[]{:S(2)}, u32[]{:S(2)}) %collective-permute-start.35) | collective-permute-done | bytes 262176 | tf_op jit(solution)/shard_map/ppermute | solution.py:10
  301.6 4.9 %collective-permute-start.36 = (bf16[2,4,128,128]{3,2,0,1:T(8,128)(2,1)S(1)}, bf16[2,4,128,128]{3,2,0,1:T(8,128)(2,1)}, u32[]{:S(2)}, u32[]{:S(2)}) collective-permute-start(bf16[2,4,128,128]{3,2,0,1:T(8,128)(2,1)S(1)} %broadcast_select_fusion.4), channel_id=1, source_target_pairs={{0,28},{4,0},{8,4},{12,8},{16,12},{20,16},{24,20},{28,24},{1,29},{... | collective-permute-start | bytes 786440 | tf_op jit(solution)/shard_map/ppermute | solution.py:10
  327.3 5.5 %collective-permute-done.43 = bf16[2,4,128,128]{3,2,0,1:T(8,128)(2,1)S(1)} collective-permute-done((bf16[2,4,128,128]{3,2,0,1:T(8,128)(2,1)}, bf16[2,4,128,128]{3,2,0,1:T(8,128)(2,1)S(1)}, u32[]{:S(2)}, u32[]{:S(2)}) %collective-permute-start.43) | collective-permute-done | bytes 262176 | tf_op jit(solution)/shard_map/ppermute | solution.py:10
  333.5 5.7 %collective-permute-start.44 = (bf16[2,4,128,128]{3,2,0,1:T(8,128)(2,1)}, bf16[2,4,128,128]{3,2,0,1:T(8,128)(2,1)S(1)}, u32[]{:S(2)}, u32[]{:S(2)}) collective-permute-start(bf16[2,4,128,128]{3,2,0,1:T(8,128)(2,1)} %broadcast_select_fusion.3), channel_id=1, source_target_pairs={{0,28},{4,0},{8,4},{12,8},{16,12},{20,16},{24,20},{28,24},{1,29},{... | collective-permute-start | bytes 786440 | tf_op jit(solution)/shard_map/ppermute | solution.py:10
  355.2 6.1 %collective-permute-done.51 = bf16[2,4,128,128]{3,2,0,1:T(8,128)(2,1)S(1)} collective-permute-done((bf16[2,4,128,128]{3,2,0,1:T(8,128)(2,1)S(1)}, bf16[2,4,128,128]{3,2,0,1:T(8,128)(2,1)S(1)}, u32[]{:S(2)}, u32[]{:S(2)}) %collective-permute-start.51) | collective-permute-done | bytes 262176 | tf_op jit(solution)/shard_map/ppermute | solution.py:10
  361.3 5.0 %collective-permute-start.52 = (bf16[2,4,128,128]{3,2,0,1:T(8,128)(2,1)S(1)}, bf16[2,4,128,128]{3,2,0,1:T(8,128)(2,1)S(1)}, u32[]{:S(2)}, u32[]{:S(2)}) collective-permute-start(bf16[2,4,128,128]{3,2,0,1:T(8,128)(2,1)S(1)} %broadcast_select_fusion.2), channel_id=1, source_target_pairs={{0,28},{4,0},{8,4},{12,8},{16,12},{20,16},{24,20},{28,24},{1,29},{... | collective-permute-start | bytes 786440 | tf_op jit(solution)/shard_map/ppermute | solution.py:10
  380.2 4.6 collective-permute-done.59
  384.8 5.0 %collective-permute-start.60 = (bf16[2,4,128,128]{3,2,0,1:T(8,128)(2,1)S(1)}, bf16[2,4,128,128]{3,2,0,1:T(8,128)(2,1)S(1)}, u32[]{:S(2)}, u32[]{:S(2)}) collective-permute-start(bf16[2,4,128,128]{3,2,0,1:T(8,128)(2,1)S(1)} %broadcast_select_fusion.1), channel_id=1, source_target_pairs={{0,28},{4,0},{8,4},{12,8},{16,12},{20,16},{24,20},{28,24},{1,29},{... | collective-permute-start | bytes 786440 | tf_op jit(solution)/shard_map/ppermute | solution.py:10
  398.7 4.3 collective-permute-start.67
  404.1 5.3 %collective-permute-done.67 = bf16[2,4,128,128]{3,2,0,1:T(8,128)(2,1)S(1)} collective-permute-done((bf16[2,4,128,128]{3,2,0,1:T(8,128)(2,1)S(1)}, bf16[2,4,128,128]{3,2,0,1:T(8,128)(2,1)S(1)}, u32[]{:S(2)}, u32[]{:S(2)}) %collective-permute-start.67) | collective-permute-done | bytes 262176 | tf_op jit(solution)/shard_map/ppermute | solution.py:10
  409.5 5.2 %collective-permute-start.68 = (bf16[2,4,128,128]{3,2,0,1:T(8,128)(2,1)S(1)}, bf16[2,4,128,128]{3,2,0,1:T(8,128)(2,1)S(1)}, u32[]{:S(2)}, u32[]{:S(2)}) collective-permute-start(bf16[2,4,128,128]{3,2,0,1:T(8,128)(2,1)S(1)} %broadcast_select_fusion), channel_id=1, source_target_pairs={{0,28},{4,0},{8,4},{12,8},{16,12},{20,16},{24,20},{28,24},{1,29},{... | collective-permute-start | bytes 786440 | tf_op jit(solution)/shard_map/ppermute | solution.py:10
  423.0 54.1 %reduce-scatter.2.cloned.1.call-done = f32[1,128,128]{2,1,0:T(8,128)} async-done(((f32[4,128,128]{2,1,0:T(8,128)}), f32[1,128,128]{2,1,0:T(8,128)}) %reduce-scatter.2.cloned.1.call-update) | async-done | bytes 65552 | tf_op jit(solution)/shard_map/reduce_scatter | solution.py:71
  (320 shorter events, 253.4 us)
Async XLA Ops:
  6.5 470.5 %reduce-scatter.2.cloned.1.call-start = ((), (), s32[]{:S(2)}) async-start(), calls=%async_computation.1 | async-start | bytes 327680 | tf_op jit(solution)/shard_map/reduce_scatter | solution.py:71
  7.5 139.8 %collective-permute-start.7 = (bf16[2,4,128,128]{3,2,0,1:T(8,128)(2,1)S(1)}, bf16[2,4,128,128]{3,2,0,1:T(8,128)(2,1)S(1)}, u32[]{:S(2)}, u32[]{:S(2)}) collective-permute-start(bf16[2,4,128,128]{3,2,0,1:T(8,128)(2,1)S(1)} %bitcast.728), channel_id=1, source_target_pairs={{0,32},{32,64},{64,96},{96,128},{128,160},{160,192},{192,224},{224... | collective-permute-start | bytes 786440 | tf_op jit(solution)/shard_map/ppermute | solution.py:10
  11.7 147.3 %collective-permute-start.21 = (bf16[2,4,128,128]{3,2,0,1:T(8,128)(2,1)S(1)}, bf16[2,4,128,128]{3,2,0,1:T(8,128)(2,1)S(1)}, u32[]{:S(2)}, u32[]{:S(2)}) collective-permute-start(bf16[2,4,128,128]{3,2,0,1:T(8,128)(2,1)S(1)} %bitcast.729), channel_id=1, source_target_pairs={{0,28},{4,0},{8,4},{12,8},{16,12},{20,16},{24,20},{28,24},{1,29},{... | collective-permute-start | bytes 786440 | tf_op jit(solution)/shard_map/ppermute | solution.py:10
  22.4 13.6 %collective-permute-start = (s32[2,4]{1,0:T(2,128)S(1)}, s32[2,4]{1,0:T(2,128)S(1)}, u32[]{:S(2)}, u32[]{:S(2)}) collective-permute-start(s32[2,4]{1,0:T(2,128)S(1)} %bitcast.730), channel_id=1, source_target_pairs={{0,32},{32,64},{64,96},{96,128},{128,160},{160,192},{192,224},{224... | collective-permute-start | bytes 104 | tf_op jit(solution)/shard_map/ppermute | solution.py:10
  25.6 13.6 %collective-permute-start.14 = (s32[2,4]{1,0:T(2,128)S(1)}, s32[2,4]{1,0:T(2,128)S(1)}, u32[]{:S(2)}, u32[]{:S(2)}) collective-permute-start(s32[2,4]{1,0:T(2,128)S(1)} %bitcast.731), channel_id=1, source_target_pairs={{0,28},{4,0},{8,4},{12,8},{16,12},{20,16},{24,20},{28,24},{1,29},{... | collective-permute-start | bytes 104 | tf_op jit(solution)/shard_map/ppermute | solution.py:10
  78.8 143.1 %collective-permute-start.62 = (s32[2,4]{1,0:T(2,128)S(1)}, s32[2,4]{1,0:T(2,128)S(1)}, u32[]{:S(2)}, u32[]{:S(2)}) collective-permute-start(s32[2,4]{1,0:T(2,128)S(1)} %collective-permute-done.54), channel_id=1, source_target_pairs={{0,28},{4,0},{8,4},{12,8},{16,12},{20,16},{24,20},{28,24},{1,29},{... | collective-permute-start | bytes 104 | tf_op jit(solution)/shard_map/ppermute | solution.py:10
  147.3 16.5 %collective-permute-start.8 = (bf16[2,4,128,128]{3,2,0,1:T(8,128)(2,1)S(1)}, bf16[2,4,128,128]{3,2,0,1:T(8,128)(2,1)S(1)}, u32[]{:S(2)}, u32[]{:S(2)}) collective-permute-start(bf16[2,4,128,128]{3,2,0,1:T(8,128)(2,1)S(1)} %broadcast_select_fusion.7), channel_id=1, source_target_pairs={{0,32},{32,64},{64,96},{96,128},{128,160},{160,192},{192,224},{224... | collective-permute-start | bytes 786440 | tf_op jit(solution)/shard_map/ppermute | solution.py:10
  159.0 11.9 %collective-permute-start.29 = (bf16[2,4,128,128]{3,2,0,1:T(8,128)(2,1)S(1)}, bf16[2,4,128,128]{3,2,0,1:T(8,128)(2,1)S(1)}, u32[]{:S(2)}, u32[]{:S(2)}) collective-permute-start(bf16[2,4,128,128]{3,2,0,1:T(8,128)(2,1)S(1)} %collective-permute-done.21), channel_id=1, source_target_pairs={{0,28},{4,0},{8,4},{12,8},{16,12},{20,16},{24,20},{28,24},{1,29},{... | collective-permute-start | bytes 786440 | tf_op jit(solution)/shard_map/ppermute | solution.py:10
  163.9 13.7 %collective-permute-start.9 = (bf16[2,4,128,128]{3,2,0,1:T(8,128)(2,1)S(1)}, bf16[2,4,128,128]{3,2,0,1:T(8,128)(2,1)S(1)}, u32[]{:S(2)}, u32[]{:S(2)}) collective-permute-start(bf16[2,4,128,128]{3,2,0,1:T(8,128)(2,1)S(1)} %broadcast_select_fusion.8), channel_id=1, source_target_pairs={{0,32},{32,64},{64,96},{96,128},{128,160},{160,192},{192,224},{224... | collective-permute-start | bytes 786440 | tf_op jit(solution)/shard_map/ppermute | solution.py:10
  166.5 13.1 %collective-permute-start.55 = (s32[2,4]{1,0:T(2,128)S(1)}, s32[2,4]{1,0:T(2,128)S(1)}, u32[]{:S(2)}, u32[]{:S(2)}) collective-permute-start(s32[2,4]{1,0:T(2,128)S(1)} %collective-permute-done.49), channel_id=1, source_target_pairs={{0,288},{32,320},{64,352},{96,384},{128,416},{160,448},{192,480},{... | collective-permute-start | bytes 104 | tf_op jit(solution)/shard_map/ppermute | solution.py:10
  168.4 11.2 %collective-permute-start.56 = (s32[2,4]{1,0:T(2,128)S(1)}, s32[2,4]{1,0:T(2,128)S(1)}, u32[]{:S(2)}, u32[]{:S(2)}) collective-permute-start(s32[2,4]{1,0:T(2,128)S(1)} %collective-permute-done.49), channel_id=1, source_target_pairs={{0,32},{32,64},{64,96},{96,128},{128,160},{160,192},{192,224},{224... | collective-permute-start | bytes 104 | tf_op jit(solution)/shard_map/ppermute | solution.py:10
  171.0 13.5 %collective-permute-start.37 = (bf16[2,4,128,128]{3,2,0,1:T(8,128)(2,1)S(1)}, bf16[2,4,128,128]{3,2,0,1:T(8,128)(2,1)S(1)}, u32[]{:S(2)}, u32[]{:S(2)}) collective-permute-start(bf16[2,4,128,128]{3,2,0,1:T(8,128)(2,1)S(1)} %collective-permute-done.29), channel_id=1, source_target_pairs={{0,28},{4,0},{8,4},{12,8},{16,12},{20,16},{24,20},{28,24},{1,29},{... | collective-permute-start | bytes 786440 | tf_op jit(solution)/shard_map/ppermute | solution.py:10
  177.6 10.7 %collective-permute-start.10 = (bf16[2,4,128,128]{3,2,0,1:T(8,128)(2,1)S(1)}, bf16[2,4,128,128]{3,2,0,1:T(8,128)(2,1)S(1)}, u32[]{:S(2)}, u32[]{:S(2)}) collective-permute-start(bf16[2,4,128,128]{3,2,0,1:T(8,128)(2,1)S(1)} %broadcast_select_fusion.9), channel_id=1, source_target_pairs={{0,32},{32,64},{64,96},{96,128},{128,160},{160,192},{192,224},{224... | collective-permute-start | bytes 786440 | tf_op jit(solution)/shard_map/ppermute | solution.py:10
  184.5 14.7 %collective-permute-start.45 = (bf16[2,4,128,128]{3,2,0,1:T(8,128)(2,1)S(1)}, bf16[2,4,128,128]{3,2,0,1:T(8,128)(2,1)S(1)}, u32[]{:S(2)}, u32[]{:S(2)}) collective-permute-start(bf16[2,4,128,128]{3,2,0,1:T(8,128)(2,1)S(1)} %collective-permute-done.37), channel_id=1, source_target_pairs={{0,28},{4,0},{8,4},{12,8},{16,12},{20,16},{24,20},{28,24},{1,29},{... | collective-permute-start | bytes 786440 | tf_op jit(solution)/shard_map/ppermute | solution.py:10
  188.4 13.1 %collective-permute-start.11 = (bf16[2,4,128,128]{3,2,0,1:T(8,128)(2,1)S(1)}, bf16[2,4,128,128]{3,2,0,1:T(8,128)(2,1)S(1)}, u32[]{:S(2)}, u32[]{:S(2)}) collective-permute-start(bf16[2,4,128,128]{3,2,0,1:T(8,128)(2,1)S(1)} %broadcast_select_fusion.10), channel_id=1, source_target_pairs={{0,480},{32,0},{64,32},{96,64},{128,96},{160,128},{192,160},{224,1... | collective-permute-start | bytes 786440 | tf_op jit(solution)/shard_map/ppermute | solution.py:10
  195.3 12.8 %collective-permute-start.63 = (s32[2,4]{1,0:T(2,128)S(1)}, s32[2,4]{1,0:T(2,128)S(1)}, u32[]{:S(2)}, u32[]{:S(2)}) collective-permute-start(s32[2,4]{1,0:T(2,128)S(1)} %collective-permute-done.57), channel_id=1, source_target_pairs={{0,288},{32,320},{64,352},{96,384},{128,416},{160,448},{192,480},{... | collective-permute-start | bytes 104 | tf_op jit(solution)/shard_map/ppermute | solution.py:10
  197.2 10.9 %collective-permute-start.64 = (s32[2,4]{1,0:T(2,128)S(1)}, s32[2,4]{1,0:T(2,128)S(1)}, u32[]{:S(2)}, u32[]{:S(2)}) collective-permute-start(s32[2,4]{1,0:T(2,128)S(1)} %collective-permute-done.57), channel_id=1, source_target_pairs={{0,32},{32,64},{64,96},{96,128},{128,160},{160,192},{192,224},{224... | collective-permute-start | bytes 104 | tf_op jit(solution)/shard_map/ppermute | solution.py:10
  199.2 14.5 %collective-permute-start.53 = (bf16[2,4,128,128]{3,2,0,1:T(8,128)(2,1)S(1)}, bf16[2,4,128,128]{3,2,0,1:T(8,128)(2,1)S(1)}, u32[]{:S(2)}, u32[]{:S(2)}) collective-permute-start(bf16[2,4,128,128]{3,2,0,1:T(8,128)(2,1)S(1)} %collective-permute-done.45), channel_id=1, source_target_pairs={{0,28},{4,0},{8,4},{12,8},{16,12},{20,16},{24,20},{28,24},{1,29},{... | collective-permute-start | bytes 786440 | tf_op jit(solution)/shard_map/ppermute | solution.py:10
  201.5 17.0 %collective-permute-start.12 = (bf16[2,4,128,128]{3,2,0,1:T(8,128)(2,1)S(1)}, bf16[2,4,128,128]{3,2,0,1:T(8,128)(2,1)S(1)}, u32[]{:S(2)}, u32[]{:S(2)}) collective-permute-start(bf16[2,4,128,128]{3,2,0,1:T(8,128)(2,1)S(1)} %broadcast_select_fusion.11), channel_id=1, source_target_pairs={{0,480},{32,0},{64,32},{96,64},{128,96},{160,128},{192,160},{224,1... | collective-permute-start | bytes 786440 | tf_op jit(solution)/shard_map/ppermute | solution.py:10
  222.3 193.5 %collective-permute-start.69 = (bf16[2,4,128,128]{3,2,0,1:T(8,128)(2,1)S(1)}, bf16[2,4,128,128]{3,2,0,1:T(8,128)(2,1)S(1)}, u32[]{:S(2)}, u32[]{:S(2)}) collective-permute-start(bf16[2,4,128,128]{3,2,0,1:T(8,128)(2,1)S(1)} %collective-permute-done.61), channel_id=1, source_target_pairs={{0,28},{4,0},{8,4},{12,8},{16,12},{20,16},{24,20},{28,24},{1,29},{... | collective-permute-start | bytes 786440 | tf_op jit(solution)/shard_map/ppermute | solution.py:10
  230.0 11.6 %collective-permute-start.18 = (bf16[2,4,128,128]{3,2,0,1:T(8,128)(2,1)}, bf16[2,4,128,128]{3,2,0,1:T(8,128)(2,1)}, u32[]{:S(2)}, u32[]{:S(2)}) collective-permute-start(bf16[2,4,128,128]{3,2,0,1:T(8,128)(2,1)} %broadcast_select_fusion.13), channel_id=1, source_target_pairs={{0,288},{32,320},{64,352},{96,384},{128,416},{160,448},{192,480},{... | collective-permute-start | bytes 786440 | tf_op jit(solution)/shard_map/ppermute | solution.py:10
  232.5 11.1 %collective-permute-start.19 = (bf16[2,4,128,128]{3,2,0,1:T(8,128)(2,1)}, bf16[2,4,128,128]{3,2,0,1:T(8,128)(2,1)}, u32[]{:S(2)}, u32[]{:S(2)}) collective-permute-start(bf16[2,4,128,128]{3,2,0,1:T(8,128)(2,1)} %broadcast_select_fusion.13), channel_id=1, source_target_pairs={{0,32},{32,64},{64,96},{96,128},{128,160},{160,192},{192,224},{224... | collective-permute-start | bytes 786440 | tf_op jit(solution)/shard_map/ppermute | solution.py:10
  262.3 11.2 %collective-permute-start.27 = (bf16[2,4,128,128]{3,2,0,1:T(8,128)(2,1)}, bf16[2,4,128,128]{3,2,0,1:T(8,128)(2,1)}, u32[]{:S(2)}, u32[]{:S(2)}) collective-permute-start(bf16[2,4,128,128]{3,2,0,1:T(8,128)(2,1)} %collective-permute-done.20), channel_id=1, source_target_pairs={{0,32},{32,64},{64,96},{96,128},{128,160},{160,192},{192,224},{224... | collective-permute-start | bytes 786440 | tf_op jit(solution)/shard_map/ppermute | solution.py:10
  285.2 10.2 %collective-permute-start.34 = (bf16[2,4,128,128]{3,2,0,1:T(8,128)(2,1)}, bf16[2,4,128,128]{3,2,0,1:T(8,128)(2,1)S(1)}, u32[]{:S(2)}, u32[]{:S(2)}) collective-permute-start(bf16[2,4,128,128]{3,2,0,1:T(8,128)(2,1)} %collective-permute-done.28), channel_id=1, source_target_pairs={{0,288},{32,320},{64,352},{96,384},{128,416},{160,448},{192,480},{... | collective-permute-start | bytes 786440 | tf_op jit(solution)/shard_map/ppermute | solution.py:10
  287.1 14.4 %collective-permute-start.35 = (bf16[2,4,128,128]{3,2,0,1:T(8,128)(2,1)}, bf16[2,4,128,128]{3,2,0,1:T(8,128)(2,1)}, u32[]{:S(2)}, u32[]{:S(2)}) collective-permute-start(bf16[2,4,128,128]{3,2,0,1:T(8,128)(2,1)} %collective-permute-done.28), channel_id=1, source_target_pairs={{0,32},{32,64},{64,96},{96,128},{128,160},{160,192},{192,224},{224... | collective-permute-start | bytes 786440 | tf_op jit(solution)/shard_map/ppermute | solution.py:10
  301.6 10.7 %collective-permute-start.36 = (bf16[2,4,128,128]{3,2,0,1:T(8,128)(2,1)S(1)}, bf16[2,4,128,128]{3,2,0,1:T(8,128)(2,1)}, u32[]{:S(2)}, u32[]{:S(2)}) collective-permute-start(bf16[2,4,128,128]{3,2,0,1:T(8,128)(2,1)S(1)} %broadcast_select_fusion.4), channel_id=1, source_target_pairs={{0,28},{4,0},{8,4},{12,8},{16,12},{20,16},{24,20},{28,24},{1,29},{... | collective-permute-start | bytes 786440 | tf_op jit(solution)/shard_map/ppermute | solution.py:10
  316.2 11.1 %collective-permute-start.42 = (bf16[2,4,128,128]{3,2,0,1:T(8,128)(2,1)}, bf16[2,4,128,128]{3,2,0,1:T(8,128)(2,1)S(1)}, u32[]{:S(2)}, u32[]{:S(2)}) collective-permute-start(bf16[2,4,128,128]{3,2,0,1:T(8,128)(2,1)} %collective-permute-done.36), channel_id=1, source_target_pairs={{0,288},{32,320},{64,352},{96,384},{128,416},{160,448},{192,480},{... | collective-permute-start | bytes 786440 | tf_op jit(solution)/shard_map/ppermute | solution.py:10
  318.2 14.6 %collective-permute-start.43 = (bf16[2,4,128,128]{3,2,0,1:T(8,128)(2,1)}, bf16[2,4,128,128]{3,2,0,1:T(8,128)(2,1)S(1)}, u32[]{:S(2)}, u32[]{:S(2)}) collective-permute-start(bf16[2,4,128,128]{3,2,0,1:T(8,128)(2,1)} %collective-permute-done.36), channel_id=1, source_target_pairs={{0,32},{32,64},{64,96},{96,128},{128,160},{160,192},{192,224},{224... | collective-permute-start | bytes 786440 | tf_op jit(solution)/shard_map/ppermute | solution.py:10
  333.5 11.1 %collective-permute-start.44 = (bf16[2,4,128,128]{3,2,0,1:T(8,128)(2,1)}, bf16[2,4,128,128]{3,2,0,1:T(8,128)(2,1)S(1)}, u32[]{:S(2)}, u32[]{:S(2)}) collective-permute-start(bf16[2,4,128,128]{3,2,0,1:T(8,128)(2,1)} %broadcast_select_fusion.3), channel_id=1, source_target_pairs={{0,28},{4,0},{8,4},{12,8},{16,12},{20,16},{24,20},{28,24},{1,29},{... | collective-permute-start | bytes 786440 | tf_op jit(solution)/shard_map/ppermute | solution.py:10
  348.8 12.5 %collective-permute-start.51 = (bf16[2,4,128,128]{3,2,0,1:T(8,128)(2,1)S(1)}, bf16[2,4,128,128]{3,2,0,1:T(8,128)(2,1)S(1)}, u32[]{:S(2)}, u32[]{:S(2)}) collective-permute-start(bf16[2,4,128,128]{3,2,0,1:T(8,128)(2,1)S(1)} %collective-permute-done.44), channel_id=1, source_target_pairs={{0,32},{32,64},{64,96},{96,128},{128,160},{160,192},{192,224},{224... | collective-permute-start | bytes 786440 | tf_op jit(solution)/shard_map/ppermute | solution.py:10
  373.8 11.0 %collective-permute-start.59 = (bf16[2,4,128,128]{3,2,0,1:T(8,128)(2,1)S(1)}, bf16[2,4,128,128]{3,2,0,1:T(8,128)(2,1)S(1)}, u32[]{:S(2)}, u32[]{:S(2)}) collective-permute-start(bf16[2,4,128,128]{3,2,0,1:T(8,128)(2,1)S(1)} %collective-permute-done.52), channel_id=1, source_target_pairs={{0,32},{32,64},{64,96},{96,128},{128,160},{160,192},{192,224},{224... | collective-permute-start | bytes 786440 | tf_op jit(solution)/shard_map/ppermute | solution.py:10
  398.7 10.7 %collective-permute-start.67 = (bf16[2,4,128,128]{3,2,0,1:T(8,128)(2,1)S(1)}, bf16[2,4,128,128]{3,2,0,1:T(8,128)(2,1)S(1)}, u32[]{:S(2)}, u32[]{:S(2)}) collective-permute-start(bf16[2,4,128,128]{3,2,0,1:T(8,128)(2,1)S(1)} %collective-permute-done.60), channel_id=1, source_target_pairs={{0,32},{32,64},{64,96},{96,128},{128,160},{160,192},{192,224},{224... | collective-permute-start | bytes 786440 | tf_op jit(solution)/shard_map/ppermute | solution.py:10
  (42 other events, 443.8 us)
Sparse Core Ops, SparseCore 0:
  423.1 53.9 reduce-scatter.1
where the time goes:
time: 495 us; the launch traced here: 486 us
  starting transfers between devices  223 us (45%)
  waiting for transfers between devices  171 us (35%)
  matrix products  46.3 us (9%)
  local copies, waits for them, and re-layouts  17.2 us (3%)
  between operations  16 us (3%)
  other arithmetic  7.3 us (1%)
  blocking collectives  5.34 us (1%)
    ppermute x70, starting transfers between devices, shifted(): return lax.ppermute(value, axis, pairs)  223 us
    ppermute x70, waiting for transfers between devices, shifted(): return lax.ppermute(value, axis, pairs)  117 us
    reduce_scatter x1, waiting for transfers between devices, on_device(): lax.psum_scatter(partial_value, 'depth', scatter_dimension=0, tiled=True)  54.1 us
    dot_general x32, matrix products, accumulate(): jnp.dot(select, blocks.reshape(slot_total, -1), precision=lax.Precision.H...  24.1 us
    dot_general x32, matrix products, accumulate(): jnp.einsum('ksab,kcb->ksac', left_vals, partner_slot, preferred_element_t...  22.2 us
  transfers between devices with their start and end apart: 71, of which 41 were waited for; matrix products, arithmetic and copies ran while one was open for 13% of the time, Pallas kernels for 0%

commit v1 on v0

v1 whole, which is shorter than its diff:
```python
import jax
import jax.numpy as jnp
from jax import lax
from jax.experimental import pallas as pl
from jax.experimental.pallas import tpu as pltpu
from jax.sharding import PartitionSpec as P

TILES = ((2, -2), (1, -2), (0, -2), (0, -1), (0, 0), (0, 1), (0, 2), (-1, 2))

LEVELS = 32766.0
TAIL = 8


def dense_kernel(rows_ref, vals_ref, out_ref):
    width = vals_ref.shape[-1]
    for column in range(vals_ref.shape[0]):
        for row in range(out_ref.shape[0]):
            slot = jnp.int32(-1)
            for candidate in range(vals_ref.shape[1]):
                slot = jnp.where(rows_ref[column, candidate] == row, candidate, slot)
            lanes = slice(column * width, (column + 1) * width)

            @pl.when(slot >= 0)
            def _():
                out_ref[row, :, lanes] = vals_ref[column, slot]

            @pl.when(slot < 0)
            def _():
                out_ref[row, :, lanes] = jnp.zeros(vals_ref.shape[2:], out_ref.dtype)


def densify(x_vals, x_rows):
    columns, slots, size, width = x_vals.shape
    return pl.pallas_call(
        dense_kernel,
        out_shape=jax.ShapeDtypeStruct((slots, size, columns * width), x_vals.dtype),
        in_specs=[pl.BlockSpec(memory_space=pltpu.SMEM), pl.BlockSpec(memory_space=pltpu.VMEM)],
        out_specs=pl.BlockSpec(memory_space=pltpu.VMEM),
    )(x_rows, x_vals)


def step_of(exponent, mantissa):
    return mantissa.astype(jnp.float32) * jnp.exp2((exponent - 14).astype(jnp.float32)) * (1.0 / LEVELS)


def encode(value, code_ref):
    size = value.shape[0]
    peak = jnp.maximum(jnp.max(jnp.abs(value), axis=0, keepdims=True), 1e-30)
    exponent = jnp.ceil(jnp.log2(peak))
    mantissa = jnp.ceil(peak * jnp.exp2(14.0 - exponent)) + 1.0
    exponent = exponent.astype(jnp.int32)
    mantissa = mantissa.astype(jnp.int32)
    code = jnp.floor(value * (1.0 / step_of(exponent, mantissa)) + 0.5)
    code_ref[:size] = code.astype(jnp.int32).astype(jnp.int16)
    line = lax.broadcasted_iota(jnp.int32, (TAIL, value.shape[1]), 0)
    tail = jnp.where(line == 0, exponent, jnp.where(line == 1, mantissa, 0))
    code_ref[size:] = tail.astype(jnp.int16)


def decode_sum_kernel(code_ref, out_ref):
    size = out_ref.shape[0]
    total = None
    for part in range(code_ref.shape[0]):
        tail = code_ref[part, size:].astype(jnp.int32)
        value = code_ref[part, :size].astype(jnp.int32).astype(jnp.float32) * step_of(tail[0:1], tail[1:2])
        total = value if total is None else total + value
    out_ref[...] = total.astype(out_ref.dtype)


def decode_sum(codes):
    size = codes.shape[2]
    vmem = pl.BlockSpec(memory_space=pltpu.VMEM)
    return pl.pallas_call(
        decode_sum_kernel,
        out_shape=jax.ShapeDtypeStruct((size, size), jnp.bfloat16),
        in_specs=[vmem],
        out_specs=vmem,
    )(codes)


def gram_kernel(positions_ref, own, own_other, below, above, near_other, below2, above2, far_other, out_ref):
    halves = {
        0: (own, own_other),
        -1: (below, near_other.at[0]),
        1: (above, near_other.at[1]),
        -2: (below2, far_other.at[0]),
        2: (above2, far_other.at[1]),
    }
    for tile, (left, right) in enumerate(TILES):
        for chip in range(out_ref.shape[1]):
            position = positions_ref[tile, chip]
            left_row = lax.shift_right_logical(position, 2)
            right_row = lax.bitwise_and(position, 3)
            total = None
            for left_ref, right_ref in zip(halves[left], halves[right]):
                product = lax.dot_general(
                    left_ref[left_row],
                    right_ref[right_row],
                    (((1,), (1,)), ((), ())),
                    preferred_element_type=jnp.float32,
                )
                total = product if total is None else total + product
            encode(total, out_ref.at[tile, chip])


def gram_blocks(positions, items):
    size = items[0].shape[1]
    vmem = pl.BlockSpec(memory_space=pltpu.VMEM)
    return pl.pallas_call(
        gram_kernel,
        out_shape=jax.ShapeDtypeStruct(positions.shape + (size + TAIL, size), jnp.int16),
        in_specs=[pl.BlockSpec(memory_space=pltpu.SMEM)] + [vmem] * len(items),
        out_specs=vmem,
        compiler_params=pltpu.CompilerParams(vmem_limit_bytes=48 * 2**20),
    )(positions, *items)


def moved(value, axis, target):
    count = lax.axis_size(axis)
    return lax.ppermute(value, axis, [(source, target(source)) for source in range(count)])


def on_device(x_vals, x_rows, out_block):
    row_count = lax.axis_size("row")
    col_count = lax.axis_size("col")
    chip_count = lax.axis_size("chip")

    def up(value):
        return moved(value, "row", lambda r: (r + 1) % row_count)

    def down(value):
        return moved(value, "row", lambda r: (r - 1) % row_count)

    def swap_core(value):
        return moved(value, "core", lambda c: c ^ 1)

    def to_worker(place):
        row, col = divmod(place, col_count)
        return (row - TILES[col][0]) % row_count * col_count + col

    def to_home(place):
        row, col = divmod(place, col_count)
        return (row + TILES[col][0]) % row_count * col_count + col

    wanted = moved(out_block.reshape(1), ("row", "col"), to_worker)
    own = densify(x_vals[0], x_rows[0])
    own, wanted = lax.optimization_barrier((own, wanted))
    below = up(own)
    above = down(own)
    spread = jnp.broadcast_to(wanted.reshape(1, 1), (col_count * chip_count, 128))
    late_own, spread = lax.optimization_barrier((own, spread))
    own_other = swap_core(late_own)
    positions = lax.all_to_all(spread, ("col", "chip"), 0, 0, tiled=True)
    positions = positions[:, 0].reshape(col_count, chip_count)
    below, above, own_other, positions = lax.optimization_barrier((below, above, own_other, positions))
    below2 = up(below)
    above2 = down(above)
    near_other = swap_core(jnp.stack([below, above]))
    far_other = swap_core(jnp.stack([below2, above2]))
    partial_sums = gram_blocks(
        positions, (own, own_other, below, above, near_other, below2, above2, far_other)
    )
    partial_sums = partial_sums.reshape((-1,) + partial_sums.shape[2:])
    gathered = lax.all_to_all(partial_sums, ("col", "chip"), 0, 0, tiled=True)
    total = decode_sum(gathered)
    result = moved(total, ("row", "col"), to_home)
    return result.reshape(out_block.shape + x_vals.shape[3:])


def solution(mesh):
    shape = dict(mesh.shape)
    devices = mesh.devices.reshape(shape["row"], shape["col"], shape["depth"] // 2, 2)
    fine_mesh = jax.sharding.Mesh(devices, ("row", "col", "chip", "core"))
    depth = ("chip", "core")
    in_specs = (
        P("row", ("col",) + depth, None, None, None),
        P("row", ("col",) + depth, None),
        P("row", "col", depth),
    )
    out_specs = P("row", "col", depth, None, None)
    return jax.shard_map(
        on_device, mesh=fine_mesh, in_specs=in_specs, out_specs=out_specs, check_vma=False
    )
```

time: 495 us -> 93 us (0.19)
  the two profiles are of different devices: /device:TPU:1 before, /device:TPU:8 now
where the time goes in v1:
time: 93 us; the launch traced here: 92.5 us
  blocking collectives  39.8 us (43%)
  starting transfers between devices  32 us (34%)
  waiting for transfers between devices  14.1 us (15%)
  Pallas kernels  5.01 us (5%)
  local copies, waits for them, and re-layouts  1.43 us (2%)
    ppermute x9, starting transfers between devices, moved(): lax.ppermute(value, axis, [(source, target(source)) for source in range(c...  32 us
    all_to_all x1, blocking collectives, on_device(): gathered = lax.all_to_all(partial_sums, ('col', 'chip'), 0, 0, tiled=True)  22.8 us
    all_to_all x1, blocking collectives, on_device(): positions = lax.all_to_all(spread, ('col', 'chip'), 0, 0, tiled=True)  17 us
    ppermute x9, waiting for transfers between devices, moved(): lax.ppermute(value, axis, [(source, target(source)) for source in range(c...  14.1 us
  transfers between devices with their start and end apart: 9, of which 4 were waited for; matrix products, arithmetic and copies ran while one was open for 0% of the time, Pallas kernels for 2%

profile of v1, /device:TPU:8, one launch (start us, length us, event | category | flops | bytes accessed | tf_op | source)
XLA Modules:
  0.0 92.5 jit_solution(6497987954291173199)
XLA Ops:
  0.0 7.7 %collective-permute-start = (s32[1]{0:T(128)}, s32[1]{0:T(128)}, u32[]{:S(2)}, u32[]{:S(2)}) collective-permute-start(s32[1]{0:T(128)} %bitcast.2), channel_id=1, source_target_pairs={{0,448},{4,484},{8,8},{12,12},{16,16},{20,20},{24,24},{28,60},{32,... | collective-permute-start | bytes 20 | tf_op jit(solution)/shard_map/ppermute | solution.py:120
  7.7 1.8 %shard_map.37.own = bf16[4,128,256]{2,1,0:T(8,128)(2,1)} custom-call(s32[2,4]{1,0:T(2,128)} %bitcast.21, bf16[2,4,128,128]{3,2,1,0:T(8,128)(2,1)} %bitcast.17), custom_call_target="tpu_custom_call" | custom-call | tf_op jit(solution)/shard_map/pallas_call | solution.py:34
  9.5 0.0 collective-permute-done
  9.5 0.6 broadcast_in_dim.8
  10.2 1.9 %collective-permute-start.3 = (bf16[4,128,256]{2,1,0:T(8,128)(2,1)}, bf16[4,128,256]{2,1,0:T(8,128)(2,1)S(1)}, u32[]{:S(2)}, u32[]{:S(2)}) collective-permute-start(bf16[4,128,256]{2,1,0:T(8,128)(2,1)} %shard_map.37.own), channel_id=1, source_target_pairs={{0,1},{1,0},{2,3},{3,2},{4,5},{5,4},{6,7},{7,6},{8,9},{9,8},{10,11... | collective-permute-start | bytes 786440 | tf_op jit(solution)/shard_map/ppermute | solution.py:120
  12.1 4.6 %collective-permute-start.2 = (bf16[4,128,256]{2,1,0:T(8,128)(2,1)}, bf16[4,128,256]{2,1,0:T(8,128)(2,1)S(1)}, u32[]{:S(2)}, u32[]{:S(2)}) collective-permute-start(bf16[4,128,256]{2,1,0:T(8,128)(2,1)} %shard_map.37.own), channel_id=1, source_target_pairs={{0,480},{32,0},{64,32},{96,64},{128,96},{160,128},{192,160},{224,1... | collective-permute-start | bytes 786440 | tf_op jit(solution)/shard_map/ppermute | solution.py:120
  16.7 1.9 %collective-permute-start.1 = (bf16[4,128,256]{2,1,0:T(8,128)(2,1)}, bf16[4,128,256]{2,1,0:T(8,128)(2,1)S(1)}, u32[]{:S(2)}, u32[]{:S(2)}) collective-permute-start(bf16[4,128,256]{2,1,0:T(8,128)(2,1)} %shard_map.37.own), channel_id=1, source_target_pairs={{0,32},{32,64},{64,96},{96,128},{128,160},{160,192},{192,224},{224... | collective-permute-start | bytes 786440 | tf_op jit(solution)/shard_map/ppermute | solution.py:120
  18.6 17.0 %all_to_all.17 = s32[16,1,128]{2,1,0:T(1,128)S(1)} all-to-all(s32[16,1,128]{2,1,0:T(1,128)S(1)} %bitcast.19), channel_id=1, replica_groups=mesh['row'=16,'col'=8,'chip'=2,'core'=2] {'col','chip'}, dimensions={0} | all-to-all | bytes 16384 | tf_op jit(solution)/shard_map/all_to_all | solution.py:153
  35.6 0.1 slice_reduce_fusion
  35.7 0.1 reshape_squeeze.3.positions_ref
  35.8 0.0 collective-permute-done.3.own_other
  35.8 0.0 collective-permute-done.2.above
  35.8 0.0 collective-permute-done.1.below
  35.8 2.0 %collective-permute-start.5 = (bf16[4,128,256]{2,1,0:T(8,128)(2,1)S(1)}, bf16[4,128,256]{2,1,0:T(8,128)(2,1)S(1)}, u32[]{:S(2)}, u32[]{:S(2)}) collective-permute-start(bf16[4,128,256]{2,1,0:T(8,128)(2,1)S(1)} %collective-permute-done.1.below), channel_id=1, source_target_pairs={{0,32},{32,64},{64,96},{96,128},{128,160},{160,192},{192,224},{224... | collective-permute-start | bytes 786440 | tf_op jit(solution)/shard_map/ppermute | solution.py:120
  37.8 3.9 %collective-permute-start.6 = (bf16[4,128,256]{2,1,0:T(8,128)(2,1)S(1)}, bf16[4,128,256]{2,1,0:T(8,128)(2,1)S(1)}, u32[]{:S(2)}, u32[]{:S(2)}) collective-permute-start(bf16[4,128,256]{2,1,0:T(8,128)(2,1)S(1)} %collective-permute-done.2.above), channel_id=1, source_target_pairs={{0,480},{32,0},{64,32},{96,64},{128,96},{160,128},{192,160},{224,1... | collective-permute-start | bytes 786440 | tf_op jit(solution)/shard_map/ppermute | solution.py:120
  41.7 0.1 pad_maximum_fusion
  41.8 1.9 %collective-permute-start.4 = (bf16[2,4,128,256]{3,2,1,0:T(8,128)(2,1)S(1)}, bf16[2,4,128,256]{3,2,1,0:T(8,128)(2,1)S(1)}, u32[]{:S(2)}, u32[]{:S(2)}) collective-permute-start(bf16[2,4,128,256]{3,2,1,0:T(8,128)(2,1)S(1)} %pad_maximum_fusion), channel_id=1, source_target_pairs={{0,1},{1,0},{2,3},{3,2},{4,5},{5,4},{6,7},{7,6},{8,9},{9,8},{10,11... | collective-permute-start | bytes 1572872 | tf_op jit(solution)/shard_map/ppermute | solution.py:120
  43.7 1.0 %collective-permute-done.5.below2 = bf16[4,128,256]{2,1,0:T(8,128)(2,1)S(1)} collective-permute-done((bf16[4,128,256]{2,1,0:T(8,128)(2,1)S(1)}, bf16[4,128,256]{2,1,0:T(8,128)(2,1)S(1)}, u32[]{:S(2)}, u32[]{:S(2)}) %collective-permute-start.5) | collective-permute-done | bytes 262176 | tf_op jit(solution)/shard_map/ppermute | solution.py:120
  44.7 3.0 %collective-permute-done.6.above2 = bf16[4,128,256]{2,1,0:T(8,128)(2,1)S(1)} collective-permute-done((bf16[4,128,256]{2,1,0:T(8,128)(2,1)S(1)}, bf16[4,128,256]{2,1,0:T(8,128)(2,1)S(1)}, u32[]{:S(2)}, u32[]{:S(2)}) %collective-permute-start.6) | collective-permute-done | bytes 262176 | tf_op jit(solution)/shard_map/ppermute | solution.py:120
  47.7 0.0 copy-start
  47.7 0.1 pad_maximum_fusion.1
  47.8 2.1 %collective-permute-start.7 = (bf16[2,4,128,256]{3,2,1,0:T(8,128)(2,1)S(1)}, bf16[2,4,128,256]{3,2,1,0:T(8,128)(2,1)S(1)}, u32[]{:S(2)}, u32[]{:S(2)}) collective-permute-start(bf16[2,4,128,256]{3,2,1,0:T(8,128)(2,1)S(1)} %pad_maximum_fusion.1), channel_id=1, source_target_pairs={{0,1},{1,0},{2,3},{3,2},{4,5},{5,4},{6,7},{7,6},{8,9},{9,8},{10,11... | collective-permute-start | bytes 1572872 | tf_op jit(solution)/shard_map/ppermute | solution.py:120
  49.8 0.0 collective-permute-done.4.near_other
  49.9 1.9 %collective-permute-done.7.far_other = bf16[2,4,128,256]{3,2,1,0:T(8,128)(2,1)S(1)} collective-permute-done((bf16[2,4,128,256]{3,2,1,0:T(8,128)(2,1)S(1)}, bf16[2,4,128,256]{3,2,1,0:T(8,128)(2,1)S(1)}, u32[]{:S(2)}, u32[]{:S(2)}) %collective-permute-start.7) | collective-permute-done | bytes 524320 | tf_op jit(solution)/shard_map/ppermute | solution.py:120
  51.7 0.0 copy-done
  51.7 1.4 %shard_map.38 = s16[8,2,136,128]{3,2,1,0:T(8,128)(2,1)S(1)} custom-call(s32[8,2]{1,0:T(8,128)S(1)} %reshape_squeeze.3.positions_ref, bf16[4,128,256]{2,1,0:T(8,128)(2,1)S(1)} %copy-done, bf16[4,128,256]{2,1,0:T(8,128)(2,1)S(1)} %collective-permute-done.3.own_other, bf16[4,128,256]{2,1,0:T(8,128)(2,1)S(1)} %collective-permute-done.1.below, ...), custom_call_target="tpu_custom_call" | custom-call | tf_op jit(solution)/shard_map/pallas_call | solution.py:109
  53.1 22.8 %all_to_all.18.code_ref = s16[16,136,128]{2,1,0:T(8,128)(2,1)} all-to-all(s16[16,136,128]{2,1,0:T(8,128)(2,1)S(1)} %bitcast.12), channel_id=1, replica_groups=mesh['row'=16,'col'=8,'chip'=2,'core'=2] {'col','chip'}, dimensions={0} | all-to-all | bytes 1114112 | tf_op jit(solution)/shard_map/all_to_all | solution.py:164
  75.9 1.8 %shard_map.39 = bf16[128,128]{1,0:T(8,128)(2,1)} custom-call(s16[16,136,128]{2,1,0:T(8,128)(2,1)} %all_to_all.18.code_ref), custom_call_target="tpu_custom_call" | custom-call | tf_op jit(solution)/shard_map/pallas_call | solution.py:73
  77.7 6.0 %collective-permute-start.8 = (bf16[128,128]{1,0:T(8,128)(2,1)}, bf16[128,128]{1,0:T(8,128)(2,1)S(1)}, u32[]{:S(2)}, u32[]{:S(2)}) collective-permute-start(bf16[128,128]{1,0:T(8,128)(2,1)} %shard_map.39), channel_id=1, source_target_pairs={{0,64},{4,36},{8,8},{12,12},{16,16},{20,20},{24,24},{28,508},{32,9... | collective-permute-start | bytes 98312 | tf_op jit(solution)/shard_map/ppermute | solution.py:120
  83.7 8.1 %collective-permute-done.8 = bf16[128,128]{1,0:T(8,128)(2,1)S(1)} collective-permute-done((bf16[128,128]{1,0:T(8,128)(2,1)}, bf16[128,128]{1,0:T(8,128)(2,1)S(1)}, u32[]{:S(2)}, u32[]{:S(2)}) %collective-permute-start.8) | collective-permute-done | bytes 32800 | tf_op jit(solution)/shard_map/ppermute | solution.py:120
  91.9 0.6 copy.5
Async XLA Ops:
  0.0 9.5 %collective-permute-start = (s32[1]{0:T(128)}, s32[1]{0:T(128)}, u32[]{:S(2)}, u32[]{:S(2)}) collective-permute-start(s32[1]{0:T(128)} %bitcast.2), channel_id=1, source_target_pairs={{0,448},{4,484},{8,8},{12,12},{16,16},{20,20},{24,24},{28,60},{32,... | collective-permute-start | bytes 20 | tf_op jit(solution)/shard_map/ppermute | solution.py:120
  10.2 25.7 %collective-permute-start.3 = (bf16[4,128,256]{2,1,0:T(8,128)(2,1)}, bf16[4,128,256]{2,1,0:T(8,128)(2,1)S(1)}, u32[]{:S(2)}, u32[]{:S(2)}) collective-permute-start(bf16[4,128,256]{2,1,0:T(8,128)(2,1)} %shard_map.37.own), channel_id=1, source_target_pairs={{0,1},{1,0},{2,3},{3,2},{4,5},{5,4},{6,7},{7,6},{8,9},{9,8},{10,11... | collective-permute-start | bytes 786440 | tf_op jit(solution)/shard_map/ppermute | solution.py:120
  12.1 23.7 %collective-permute-start.2 = (bf16[4,128,256]{2,1,0:T(8,128)(2,1)}, bf16[4,128,256]{2,1,0:T(8,128)(2,1)S(1)}, u32[]{:S(2)}, u32[]{:S(2)}) collective-permute-start(bf16[4,128,256]{2,1,0:T(8,128)(2,1)} %shard_map.37.own), channel_id=1, source_target_pairs={{0,480},{32,0},{64,32},{96,64},{128,96},{160,128},{192,160},{224,1... | collective-permute-start | bytes 786440 | tf_op jit(solution)/shard_map/ppermute | solution.py:120
  16.7 19.1 %collective-permute-start.1 = (bf16[4,128,256]{2,1,0:T(8,128)(2,1)}, bf16[4,128,256]{2,1,0:T(8,128)(2,1)S(1)}, u32[]{:S(2)}, u32[]{:S(2)}) collective-permute-start(bf16[4,128,256]{2,1,0:T(8,128)(2,1)} %shard_map.37.own), channel_id=1, source_target_pairs={{0,32},{32,64},{64,96},{96,128},{128,160},{160,192},{192,224},{224... | collective-permute-start | bytes 786440 | tf_op jit(solution)/shard_map/ppermute | solution.py:120
  35.8 8.9 %collective-permute-start.5 = (bf16[4,128,256]{2,1,0:T(8,128)(2,1)S(1)}, bf16[4,128,256]{2,1,0:T(8,128)(2,1)S(1)}, u32[]{:S(2)}, u32[]{:S(2)}) collective-permute-start(bf16[4,128,256]{2,1,0:T(8,128)(2,1)S(1)} %collective-permute-done.1.below), channel_id=1, source_target_pairs={{0,32},{32,64},{64,96},{96,128},{128,160},{160,192},{192,224},{224... | collective-permute-start | bytes 786440 | tf_op jit(solution)/shard_map/ppermute | solution.py:120
  37.8 9.9 %collective-permute-start.6 = (bf16[4,128,256]{2,1,0:T(8,128)(2,1)S(1)}, bf16[4,128,256]{2,1,0:T(8,128)(2,1)S(1)}, u32[]{:S(2)}, u32[]{:S(2)}) collective-permute-start(bf16[4,128,256]{2,1,0:T(8,128)(2,1)S(1)} %collective-permute-done.2.above), channel_id=1, source_target_pairs={{0,480},{32,0},{64,32},{96,64},{128,96},{160,128},{192,160},{224,1... | collective-permute-start | bytes 786440 | tf_op jit(solution)/shard_map/ppermute | solution.py:120
  41.8 8.1 %collective-permute-start.4 = (bf16[2,4,128,256]{3,2,1,0:T(8,128)(2,1)S(1)}, bf16[2,4,128,256]{3,2,1,0:T(8,128)(2,1)S(1)}, u32[]{:S(2)}, u32[]{:S(2)}) collective-permute-start(bf16[2,4,128,256]{3,2,1,0:T(8,128)(2,1)S(1)} %pad_maximum_fusion), channel_id=1, source_target_pairs={{0,1},{1,0},{2,3},{3,2},{4,5},{5,4},{6,7},{7,6},{8,9},{9,8},{10,11... | collective-permute-start | bytes 1572872 | tf_op jit(solution)/shard_map/ppermute | solution.py:120
  47.7 4.0 %copy-start = (bf16[4,128,256]{2,1,0:T(8,128)(2,1)S(1)}, bf16[4,128,256]{2,1,0:T(8,128)(2,1)}, u32[]{:S(2)}) copy-start(bf16[4,128,256]{2,1,0:T(8,128)(2,1)} %shard_map.37.own) | copy-start | bytes 786436
  47.8 3.9 %collective-permute-start.7 = (bf16[2,4,128,256]{3,2,1,0:T(8,128)(2,1)S(1)}, bf16[2,4,128,256]{3,2,1,0:T(8,128)(2,1)S(1)}, u32[]{:S(2)}, u32[]{:S(2)}) collective-permute-start(bf16[2,4,128,256]{3,2,1,0:T(8,128)(2,1)S(1)} %pad_maximum_fusion.1), channel_id=1, source_target_pairs={{0,1},{1,0},{2,3},{3,2},{4,5},{5,4},{6,7},{7,6},{8,9},{9,8},{10,11... | collective-permute-start | bytes 1572872 | tf_op jit(solution)/shard_map/ppermute | solution.py:120
  77.7 14.2 %collective-permute-start.8 = (bf16[128,128]{1,0:T(8,128)(2,1)}, bf16[128,128]{1,0:T(8,128)(2,1)S(1)}, u32[]{:S(2)}, u32[]{:S(2)}) collective-permute-start(bf16[128,128]{1,0:T(8,128)(2,1)} %shard_map.39), channel_id=1, source_target_pairs={{0,64},{4,36},{8,8},{12,12},{16,16},{20,20},{24,24},{28,508},{32,9... | collective-permute-start | bytes 98312 | tf_op jit(solution)/shard_map/ppermute | solution.py:120

commit v2 on v1

--- a/solution.py
+++ b/solution.py
@@ -9,34 +9,40 @@
 
 LEVELS = 32766.0
 TAIL = 8
+NOTE = 16
 
 
-def dense_kernel(rows_ref, vals_ref, out_ref):
-    width = vals_ref.shape[-1]
-    for column in range(vals_ref.shape[0]):
-        for row in range(out_ref.shape[0]):
+def dense_kernel(rows_ref, wanted_ref, vals_ref, out_ref):
+    columns, slots, size, width = vals_ref.shape
+    for column in range(columns):
+        for row in range(slots):
             slot = jnp.int32(-1)
-            for candidate in range(vals_ref.shape[1]):
+            for candidate in range(slots):
                 slot = jnp.where(rows_ref[column, candidate] == row, candidate, slot)
-            lanes = slice(column * width, (column + 1) * width)
+            at = (slice(row * size, (row + 1) * size), slice(column * width, (column + 1) * width))
 
             @pl.when(slot >= 0)
             def _():
-                out_ref[row, :, lanes] = vals_ref[column, slot]
+                out_ref[at] = vals_ref[column, slot]
 
             @pl.when(slot < 0)
             def _():
-                out_ref[row, :, lanes] = jnp.zeros(vals_ref.shape[2:], out_ref.dtype)
+                out_ref[at] = jnp.zeros((size, width), out_ref.dtype)
+
+    note = jnp.full((NOTE, columns * width), wanted_ref[0], jnp.int32)
+    out_ref[slots * size :] = note.astype(jnp.float32).astype(out_ref.dtype)
 
 
-def densify(x_vals, x_rows):
+def densify(x_vals, x_rows, wanted):
     columns, slots, size, width = x_vals.shape
+    smem = pl.BlockSpec(memory_space=pltpu.SMEM)
+    vmem = pl.BlockSpec(memory_space=pltpu.VMEM)
     return pl.pallas_call(
         dense_kernel,
-        out_shape=jax.ShapeDtypeStruct((slots, size, columns * width), x_vals.dtype),
-        in_specs=[pl.BlockSpec(memory_space=pltpu.SMEM), pl.BlockSpec(memory_space=pltpu.VMEM)],
-        out_specs=pl.BlockSpec(memory_space=pltpu.VMEM),
-    )(x_rows, x_vals)
+        out_shape=jax.ShapeDtypeStruct((slots * size + NOTE, columns * width), x_vals.dtype),
+        in_specs=[smem, smem, vmem],
+        out_specs=vmem,
+    )(x_rows, wanted, x_vals)
 
 
 def step_of(exponent, mantissa):
@@ -78,24 +84,25 @@
     )(codes)
 
 
-def gram_kernel(positions_ref, own, own_other, below, above, near_other, below2, above2, far_other, out_ref):
+def gram_kernel(positions_ref, own, own_other, below, above, near_other, below2, above2, below2_other, above2_other, out_ref):
     halves = {
         0: (own, own_other),
         -1: (below, near_other.at[0]),
         1: (above, near_other.at[1]),
-        -2: (below2, far_other.at[0]),
-        2: (above2, far_other.at[1]),
+        -2: (below2, below2_other),
+        2: (above2, above2_other),
     }
     for tile, (left, right) in enumerate(TILES):
         for chip in range(out_ref.shape[1]):
             position = positions_ref[tile, chip]
-            left_row = lax.shift_right_logical(position, 2)
-            right_row = lax.bitwise_and(position, 3)
+            size = out_ref.shape[3]
+            left_row = pl.ds(pl.multiple_of(lax.shift_right_logical(position, 2) * size, size), size)
+            right_row = pl.ds(pl.multiple_of(lax.bitwise_and(position, 3) * size, size), size)
             total = None
             for left_ref, right_ref in zip(halves[left], halves[right]):
                 product = lax.dot_general(
-                    left_ref[left_row],
-                    right_ref[right_row],
+                    left_ref[left_row, :],
+                    right_ref[right_row, :],
                     (((1,), (1,)), ((), ())),
                     preferred_element_type=jnp.float32,
                 )
@@ -103,8 +110,7 @@
             encode(total, out_ref.at[tile, chip])
 
 
-def gram_blocks(positions, items):
-    size = items[0].shape[1]
+def gram_blocks(positions, items, size):
     vmem = pl.BlockSpec(memory_space=pltpu.VMEM)
     return pl.pallas_call(
         gram_kernel,
@@ -134,31 +140,32 @@
     def swap_core(value):
         return moved(value, "core", lambda c: c ^ 1)
 
-    def to_worker(place):
-        row, col = divmod(place, col_count)
-        return (row - TILES[col][0]) % row_count * col_count + col
-
     def to_home(place):
         row, col = divmod(place, col_count)
         return (row + TILES[col][0]) % row_count * col_count + col
 
-    wanted = moved(out_block.reshape(1), ("row", "col"), to_worker)
-    own = densify(x_vals[0], x_rows[0])
-    own, wanted = lax.optimization_barrier((own, wanted))
+    own = densify(x_vals[0], x_rows[0], out_block.reshape(1))
     below = up(own)
     above = down(own)
-    spread = jnp.broadcast_to(wanted.reshape(1, 1), (col_count * chip_count, 128))
-    late_own, spread = lax.optimization_barrier((own, spread))
-    own_other = swap_core(late_own)
-    positions = lax.all_to_all(spread, ("col", "chip"), 0, 0, tiled=True)
-    positions = positions[:, 0].reshape(col_count, chip_count)
-    below, above, own_other, positions = lax.optimization_barrier((below, above, own_other, positions))
     below2 = up(below)
     above2 = down(above)
-    near_other = swap_core(jnp.stack([below, above]))
-    far_other = swap_core(jnp.stack([below2, above2]))
+    late_own, near = lax.optimization_barrier((own, jnp.stack([below, above])))
+    near_other = swap_core(near)
+    own_other = swap_core(late_own)
+    above2_other = swap_core(above2)
+    col = lax.axis_index("col")
+    wanted = own[-1, :128]
+    for shift, item in ((2, above2), (1, above), (-1, below)):
+        for tile, (left, _) in enumerate(TILES):
+            if left == shift:
+                wanted = jnp.where(col == tile, item[-1, :128], wanted)
+    spread = jnp.broadcast_to(wanted.astype(jnp.float32), (col_count * chip_count, 128))
+    gathered_positions = lax.all_to_all(spread, ("col", "chip"), 0, 0, tiled=True)
+    below2, gathered_positions = lax.optimization_barrier((below2, gathered_positions))
+    positions = gathered_positions[:, 0].astype(jnp.int32).reshape(col_count, chip_count)
+    below2_other = swap_core(below2)
     partial_sums = gram_blocks(
-        positions, (own, own_other, below, above, near_other, below2, above2, far_other)
+        positions, (own, own_other, below, above, near_other, below2, above2, below2_other, above2_other), x_vals.shape[3]
     )
     partial_sums = partial_sums.reshape((-1,) + partial_sums.shape[2:])
     gathered = lax.all_to_all(partial_sums, ("col", "chip"), 0, 0, tiled=True)

time: 93 us -> 90.3 us (0.971)
  blocking collectives: 39.8 us -> 23.2 us
  starting transfers between devices: 32 us -> 40.7 us
  waiting for transfers between devices: 14.1 us -> 18.6 us
    all_to_all x1 -> x0, blocking collectives: 17 us -> none  [on_device(): positions = lax.all_to_all(spread, ('col', 'chip'), 0, 0, tiled=True)]
    all_to_all x0 -> x1, starting transfers between devices: none -> 10.4 us  [on_device(): lax.all_to_all(spread, ('col', 'chip'), 0, 0, tiled=True)]
    all_to_all x0 -> x1, waiting for transfers between devices: none -> 4.07 us  [on_device(): lax.all_to_all(spread, ('col', 'chip'), 0, 0, tiled=True)]
    ppermute x9, starting transfers between devices: 32 us -> 30.3 us  [moved(): lax.ppermute(value, axis, [(source, target(source)) for source in range(c...]
  transfers between devices with their start and end apart: 9 -> 10, of which waited for: 4 -> 6; matrix products, arithmetic and copies ran while one was open for 0% -> 1% of each run, Pallas kernels for 2% -> 0%
where the time goes in v2:
time: 90.3 us; the launch traced here: 89.8 us
  starting transfers between devices  40.7 us (45%)
  blocking collectives  23.2 us (26%)
  waiting for transfers between devices  18.6 us (21%)
  Pallas kernels  5.05 us (6%)
  local copies, waits for them, and re-layouts  1.3 us (1%)
    ppermute x9, starting transfers between devices, moved(): lax.ppermute(value, axis, [(source, target(source)) for source in range(c...  30.3 us
    all_to_all x1, blocking collectives, on_device(): gathered = lax.all_to_all(partial_sums, ('col', 'chip'), 0, 0, tiled=True)  23.2 us
    ppermute x9, waiting for transfers between devices, moved(): lax.ppermute(value, axis, [(source, target(source)) for source in range(c...  14.5 us
    all_to_all x1, starting transfers between devices, on_device(): lax.all_to_all(spread, ('col', 'chip'), 0, 0, tiled=True)  10.4 us
    all_to_all x1, waiting for transfers between devices, on_device(): lax.all_to_all(spread, ('col', 'chip'), 0, 0, tiled=True)  4.07 us
    pallas_call x1, Pallas kernels, densify(): pl.pallas_call(dense_kernel, out_shape=jax.ShapeDtypeStruct((slots * size...  1.83 us
    pallas_call x1, Pallas kernels, decode_sum(): pl.pallas_call(decode_sum_kernel, out_shape=jax.ShapeDtypeStruct((size, s...  1.82 us
  transfers between devices with their start and end apart: 10, of which 6 were waited for; matrix products, arithmetic and copies ran while one was open for 1% of the time, Pallas kernels for 0%

profile of v2, /device:TPU:8, one launch (start us, length us, event | category | flops | bytes accessed | tf_op | source)
XLA Modules:
  0.0 89.8 jit_solution(7199274602515958258)
XLA Ops:
  0.7 1.8 %shard_map.37.own = bf16[528,256]{1,0:T(8,128)(2,1)} custom-call(s32[2,4]{1,0:T(2,128)} %bitcast.20, s32[1]{0:T(128)} %bitcast.13.wanted_ref, bf16[2,4,128,128]{3,2,1,0:T(8,128)(2,1)} %bitcast.17), custom_call_target="tpu_custom_call" | custom-call | tf_op jit(solution)/shard_map/pallas_call | solution.py:40
  2.5 7.7 %collective-permute-start.2 = (bf16[528,256]{1,0:T(8,128)(2,1)}, bf16[528,256]{1,0:T(8,128)(2,1)S(1)}, u32[]{:S(2)}, u32[]{:S(2)}) collective-permute-start(bf16[528,256]{1,0:T(8,128)(2,1)} %shard_map.37.own), channel_id=1, source_target_pairs={{0,480},{32,0},{64,32},{96,64},{128,96},{160,128},{192,160},{224,1... | collective-permute-start | bytes 811016 | tf_op jit(solution)/shard_map/ppermute | solution.py:126
  10.2 1.9 %collective-permute-start = (bf16[528,256]{1,0:T(8,128)(2,1)}, bf16[528,256]{1,0:T(8,128)(2,1)S(1)}, u32[]{:S(2)}, u32[]{:S(2)}) collective-permute-start(bf16[528,256]{1,0:T(8,128)(2,1)} %shard_map.37.own), channel_id=1, source_target_pairs={{0,32},{32,64},{64,96},{96,128},{128,160},{160,192},{192,224},{224... | collective-permute-start | bytes 811016 | tf_op jit(solution)/shard_map/ppermute | solution.py:126
  12.1 2.3 %collective-permute-done.2.above = bf16[528,256]{1,0:T(8,128)(2,1)S(1)} collective-permute-done((bf16[528,256]{1,0:T(8,128)(2,1)}, bf16[528,256]{1,0:T(8,128)(2,1)S(1)}, u32[]{:S(2)}, u32[]{:S(2)}) %collective-permute-start.2) | collective-permute-done | bytes 270368 | tf_op jit(solution)/shard_map/ppermute | solution.py:126
  14.5 4.3 %collective-permute-start.3 = (bf16[528,256]{1,0:T(8,128)(2,1)S(1)}, bf16[528,256]{1,0:T(8,128)(2,1)S(1)}, u32[]{:S(2)}, u32[]{:S(2)}) collective-permute-start(bf16[528,256]{1,0:T(8,128)(2,1)S(1)} %collective-permute-done.2.above), channel_id=1, source_target_pairs={{0,480},{32,0},{64,32},{96,64},{128,96},{160,128},{192,160},{224,1... | collective-permute-start | bytes 811016 | tf_op jit(solution)/shard_map/ppermute | solution.py:126
  18.8 0.3 collective-permute-done.below
  19.1 1.9 %collective-permute-start.1 = (bf16[528,256]{1,0:T(8,128)(2,1)S(1)}, bf16[528,256]{1,0:T(8,128)(2,1)S(1)}, u32[]{:S(2)}, u32[]{:S(2)}) collective-permute-start(bf16[528,256]{1,0:T(8,128)(2,1)S(1)} %collective-permute-done.below), channel_id=1, source_target_pairs={{0,32},{32,64},{64,96},{96,128},{128,160},{160,192},{192,224},{224... | collective-permute-start | bytes 811016 | tf_op jit(solution)/shard_map/ppermute | solution.py:126
  21.0 0.0 copy-start
  21.0 0.1 pad_maximum_fusion
  21.1 1.9 %collective-permute-start.5 = (bf16[2,528,256]{2,1,0:T(8,128)(2,1)S(1)}, bf16[2,528,256]{2,1,0:T(8,128)(2,1)S(1)}, u32[]{:S(2)}, u32[]{:S(2)}) collective-permute-start(bf16[2,528,256]{2,1,0:T(8,128)(2,1)S(1)} %pad_maximum_fusion), channel_id=1, source_target_pairs={{0,1},{1,0},{2,3},{3,2},{4,5},{5,4},{6,7},{7,6},{8,9},{9,8},{10,11... | collective-permute-start | bytes 1622024 | tf_op jit(solution)/shard_map/ppermute | solution.py:126
  23.0 0.5 collective-permute-done.3.above2
  23.6 0.0 copy-done
  23.6 0.6 broadcast_in_dim.3
  24.2 10.4 %all-to-all-start = ((f32[16,1,128]{2,1,0:T(1,128)}), f32[16,1,128]{2,1,0:T(1,128)S(1)}, u32[]{:S(2)}, u32[]{:S(2)}) async-start(f32[16,1,128]{2,1,0:T(1,128)} %broadcast_in_dim.3), calls=%async_computation | async-start | bytes 16384 | tf_op jit(solution)/shard_map/all_to_all | solution.py:163
  34.6 1.9 %collective-permute-start.4 = (bf16[528,256]{1,0:T(8,128)(2,1)S(1)}, bf16[528,256]{1,0:T(8,128)(2,1)S(1)}, u32[]{:S(2)}, u32[]{:S(2)}) collective-permute-start(bf16[528,256]{1,0:T(8,128)(2,1)S(1)} %copy-done), channel_id=1, source_target_pairs={{0,1},{1,0},{2,3},{3,2},{4,5},{5,4},{6,7},{7,6},{8,9},{9,8},{10,11... | collective-permute-start | bytes 811016 | tf_op jit(solution)/shard_map/ppermute | solution.py:126
  36.5 2.4 %collective-permute-start.7 = (bf16[528,256]{1,0:T(8,128)(2,1)S(1)}, bf16[528,256]{1,0:T(8,128)(2,1)S(1)}, u32[]{:S(2)}, u32[]{:S(2)}) collective-permute-start(bf16[528,256]{1,0:T(8,128)(2,1)S(1)} %collective-permute-done.3.above2), channel_id=1, source_target_pairs={{0,1},{1,0},{2,3},{3,2},{4,5},{5,4},{6,7},{7,6},{8,9},{9,8},{10,11... | collective-permute-start | bytes 811016 | tf_op jit(solution)/shard_map/ppermute | solution.py:126
  39.0 0.0 collective-permute-done.1.below2
  39.0 4.1 %all-to-all-done = f32[16,1,128]{2,1,0:T(1,128)S(1)} async-done(((f32[16,1,128]{2,1,0:T(1,128)}), f32[16,1,128]{2,1,0:T(1,128)S(1)}, u32[]{:S(2)}, u32[]{:S(2)}) %all-to-all-start) | async-done | bytes 8224 | tf_op jit(solution)/shard_map/all_to_all | solution.py:163
  43.0 1.9 %collective-permute-start.6 = (bf16[528,256]{1,0:T(8,128)(2,1)S(1)}, bf16[528,256]{1,0:T(8,128)(2,1)S(1)}, u32[]{:S(2)}, u32[]{:S(2)}) collective-permute-start(bf16[528,256]{1,0:T(8,128)(2,1)S(1)} %collective-permute-done.1.below2), channel_id=1, source_target_pairs={{0,1},{1,0},{2,3},{3,2},{4,5},{5,4},{6,7},{7,6},{8,9},{9,8},{10,11... | collective-permute-start | bytes 811016 | tf_op jit(solution)/shard_map/ppermute | solution.py:126
  45.0 0.1 convert_reduce_fusion
  45.1 0.1 convert_element_type.16.positions_ref
  45.1 0.0 collective-permute-done.4.own_other
  45.2 0.0 collective-permute-done.7.above2_other
  45.2 0.0 collective-permute-done.5.near_other
  45.2 1.3 %collective-permute-done.6.below2_other = bf16[528,256]{1,0:T(8,128)(2,1)S(1)} collective-permute-done((bf16[528,256]{1,0:T(8,128)(2,1)S(1)}, bf16[528,256]{1,0:T(8,128)(2,1)S(1)}, u32[]{:S(2)}, u32[]{:S(2)}) %collective-permute-start.6) | collective-permute-done | bytes 270368 | tf_op jit(solution)/shard_map/ppermute | solution.py:126
  46.5 1.4 %shard_map.38 = s16[8,2,136,128]{3,2,1,0:T(8,128)(2,1)S(1)} custom-call(s32[8,2]{1,0:T(8,128)S(1)} %convert_element_type.16.positions_ref, bf16[528,256]{1,0:T(8,128)(2,1)S(1)} %copy-done, bf16[528,256]{1,0:T(8,128)(2,1)S(1)} %collective-permute-done.4.own_other, bf16[528,256]{1,0:T(8,128)(2,1)S(1)} %collective-permute-done.below, ...), custom_call_target="tpu_custom_call" | custom-call | tf_op jit(solution)/shard_map/pallas_call | solution.py:115
  47.9 23.2 %all_to_all.14.code_ref = s16[16,136,128]{2,1,0:T(8,128)(2,1)} all-to-all(s16[16,136,128]{2,1,0:T(8,128)(2,1)S(1)} %bitcast.14), channel_id=1, replica_groups=mesh['row'=16,'col'=8,'chip'=2,'core'=2] {'col','chip'}, dimensions={0} | all-to-all | bytes 1114112 | tf_op jit(solution)/shard_map/all_to_all | solution.py:171
  71.1 1.8 %shard_map.39 = bf16[128,128]{1,0:T(8,128)(2,1)} custom-call(s16[16,136,128]{2,1,0:T(8,128)(2,1)} %all_to_all.14.code_ref), custom_call_target="tpu_custom_call" | custom-call | tf_op jit(solution)/shard_map/pallas_call | solution.py:79
  72.9 6.3 %collective-permute-start.8 = (bf16[128,128]{1,0:T(8,128)(2,1)}, bf16[128,128]{1,0:T(8,128)(2,1)S(1)}, u32[]{:S(2)}, u32[]{:S(2)}) collective-permute-start(bf16[128,128]{1,0:T(8,128)(2,1)} %shard_map.39), channel_id=1, source_target_pairs={{0,64},{4,36},{8,8},{12,12},{16,16},{20,20},{24,24},{28,508},{32,9... | collective-permute-start | bytes 98312 | tf_op jit(solution)/shard_map/ppermute | solution.py:126
  79.2 10.0 %collective-permute-done.8 = bf16[128,128]{1,0:T(8,128)(2,1)S(1)} collective-permute-done((bf16[128,128]{1,0:T(8,128)(2,1)}, bf16[128,128]{1,0:T(8,128)(2,1)S(1)}, u32[]{:S(2)}, u32[]{:S(2)}) %collective-permute-start.8) | collective-permute-done | bytes 32800 | tf_op jit(solution)/shard_map/ppermute | solution.py:126
  89.2 0.6 copy.6
  (1 shorter events, 0.0 us)
Async XLA Ops:
  2.5 12.0 %collective-permute-start.2 = (bf16[528,256]{1,0:T(8,128)(2,1)}, bf16[528,256]{1,0:T(8,128)(2,1)S(1)}, u32[]{:S(2)}, u32[]{:S(2)}) collective-permute-start(bf16[528,256]{1,0:T(8,128)(2,1)} %shard_map.37.own), channel_id=1, source_target_pairs={{0,480},{32,0},{64,32},{96,64},{128,96},{160,128},{192,160},{224,1... | collective-permute-start | bytes 811016 | tf_op jit(solution)/shard_map/ppermute | solution.py:126
  10.2 8.9 %collective-permute-start = (bf16[528,256]{1,0:T(8,128)(2,1)}, bf16[528,256]{1,0:T(8,128)(2,1)S(1)}, u32[]{:S(2)}, u32[]{:S(2)}) collective-permute-start(bf16[528,256]{1,0:T(8,128)(2,1)} %shard_map.37.own), channel_id=1, source_target_pairs={{0,32},{32,64},{64,96},{96,128},{128,160},{160,192},{192,224},{224... | collective-permute-start | bytes 811016 | tf_op jit(solution)/shard_map/ppermute | solution.py:126
  14.5 9.1 %collective-permute-start.3 = (bf16[528,256]{1,0:T(8,128)(2,1)S(1)}, bf16[528,256]{1,0:T(8,128)(2,1)S(1)}, u32[]{:S(2)}, u32[]{:S(2)}) collective-permute-start(bf16[528,256]{1,0:T(8,128)(2,1)S(1)} %collective-permute-done.2.above), channel_id=1, source_target_pairs={{0,480},{32,0},{64,32},{96,64},{128,96},{160,128},{192,160},{224,1... | collective-permute-start | bytes 811016 | tf_op jit(solution)/shard_map/ppermute | solution.py:126
  19.1 19.9 %collective-permute-start.1 = (bf16[528,256]{1,0:T(8,128)(2,1)S(1)}, bf16[528,256]{1,0:T(8,128)(2,1)S(1)}, u32[]{:S(2)}, u32[]{:S(2)}) collective-permute-start(bf16[528,256]{1,0:T(8,128)(2,1)S(1)} %collective-permute-done.below), channel_id=1, source_target_pairs={{0,32},{32,64},{64,96},{96,128},{128,160},{160,192},{192,224},{224... | collective-permute-start | bytes 811016 | tf_op jit(solution)/shard_map/ppermute | solution.py:126
  21.0 2.6 %copy-start = (bf16[528,256]{1,0:T(8,128)(2,1)S(1)}, bf16[528,256]{1,0:T(8,128)(2,1)}, u32[]{:S(2)}) copy-start(bf16[528,256]{1,0:T(8,128)(2,1)} %shard_map.37.own) | copy-start | bytes 811012
  21.1 24.1 %collective-permute-start.5 = (bf16[2,528,256]{2,1,0:T(8,128)(2,1)S(1)}, bf16[2,528,256]{2,1,0:T(8,128)(2,1)S(1)}, u32[]{:S(2)}, u32[]{:S(2)}) collective-permute-start(bf16[2,528,256]{2,1,0:T(8,128)(2,1)S(1)} %pad_maximum_fusion), channel_id=1, source_target_pairs={{0,1},{1,0},{2,3},{3,2},{4,5},{5,4},{6,7},{7,6},{8,9},{9,8},{10,11... | collective-permute-start | bytes 1622024 | tf_op jit(solution)/shard_map/ppermute | solution.py:126
  24.2 18.9 %all-to-all-start = ((f32[16,1,128]{2,1,0:T(1,128)}), f32[16,1,128]{2,1,0:T(1,128)S(1)}, u32[]{:S(2)}, u32[]{:S(2)}) async-start(f32[16,1,128]{2,1,0:T(1,128)} %broadcast_in_dim.3), calls=%async_computation | async-start | bytes 16384 | tf_op jit(solution)/shard_map/all_to_all | solution.py:163
  34.6 10.5 %collective-permute-start.4 = (bf16[528,256]{1,0:T(8,128)(2,1)S(1)}, bf16[528,256]{1,0:T(8,128)(2,1)S(1)}, u32[]{:S(2)}, u32[]{:S(2)}) collective-permute-start(bf16[528,256]{1,0:T(8,128)(2,1)S(1)} %copy-done), channel_id=1, source_target_pairs={{0,1},{1,0},{2,3},{3,2},{4,5},{5,4},{6,7},{7,6},{8,9},{9,8},{10,11... | collective-permute-start | bytes 811016 | tf_op jit(solution)/shard_map/ppermute | solution.py:126
  36.5 8.6 %collective-permute-start.7 = (bf16[528,256]{1,0:T(8,128)(2,1)S(1)}, bf16[528,256]{1,0:T(8,128)(2,1)S(1)}, u32[]{:S(2)}, u32[]{:S(2)}) collective-permute-start(bf16[528,256]{1,0:T(8,128)(2,1)S(1)} %collective-permute-done.3.above2), channel_id=1, source_target_pairs={{0,1},{1,0},{2,3},{3,2},{4,5},{5,4},{6,7},{7,6},{8,9},{9,8},{10,11... | collective-permute-start | bytes 811016 | tf_op jit(solution)/shard_map/ppermute | solution.py:126
  43.0 3.4 %collective-permute-start.6 = (bf16[528,256]{1,0:T(8,128)(2,1)S(1)}, bf16[528,256]{1,0:T(8,128)(2,1)S(1)}, u32[]{:S(2)}, u32[]{:S(2)}) collective-permute-start(bf16[528,256]{1,0:T(8,128)(2,1)S(1)} %collective-permute-done.1.below2), channel_id=1, source_target_pairs={{0,1},{1,0},{2,3},{3,2},{4,5},{5,4},{6,7},{7,6},{8,9},{9,8},{10,11... | collective-permute-start | bytes 811016 | tf_op jit(solution)/shard_map/ppermute | solution.py:126
  72.9 16.3 %collective-permute-start.8 = (bf16[128,128]{1,0:T(8,128)(2,1)}, bf16[128,128]{1,0:T(8,128)(2,1)S(1)}, u32[]{:S(2)}, u32[]{:S(2)}) collective-permute-start(bf16[128,128]{1,0:T(8,128)(2,1)} %shard_map.39), channel_id=1, source_target_pairs={{0,64},{4,36},{8,8},{12,12},{16,16},{20,20},{24,24},{28,508},{32,9... | collective-permute-start | bytes 98312 | tf_op jit(solution)/shard_map/ppermute | solution.py:126

commit v3 on v2

--- a/solution.py
+++ b/solution.py
@@ -7,6 +7,8 @@
 
 TILES = ((2, -2), (1, -2), (0, -2), (0, -1), (0, 0), (0, 1), (0, 2), (-1, 2))
 
+NEAR = (3, 4, 5, 6, 7)
+FAR = (0, 1, 2)
 LEVELS = 32766.0
 TAIL = 8
 NOTE = 16
@@ -84,41 +86,42 @@
     )(codes)
 
 
-def gram_kernel(positions_ref, own, own_other, below, above, near_other, below2, above2, below2_other, above2_other, out_ref):
-    halves = {
-        0: (own, own_other),
-        -1: (below, near_other.at[0]),
-        1: (above, near_other.at[1]),
-        -2: (below2, below2_other),
-        2: (above2, above2_other),
-    }
-    for tile, (left, right) in enumerate(TILES):
-        for chip in range(out_ref.shape[1]):
-            position = positions_ref[tile, chip]
-            size = out_ref.shape[3]
-            left_row = pl.ds(pl.multiple_of(lax.shift_right_logical(position, 2) * size, size), size)
-            right_row = pl.ds(pl.multiple_of(lax.bitwise_and(position, 3) * size, size), size)
-            total = None
-            for left_ref, right_ref in zip(halves[left], halves[right]):
-                product = lax.dot_general(
-                    left_ref[left_row, :],
-                    right_ref[right_row, :],
-                    (((1,), (1,)), ((), ())),
-                    preferred_element_type=jnp.float32,
-                )
-                total = product if total is None else total + product
-            encode(total, out_ref.at[tile, chip])
-
-
-def gram_blocks(positions, items, size):
+def gram_blocks(positions, tiles, items, size, done=None):
+    offsets = sorted(items)
+    ready = [] if done is None else [done]
+
+    def kernel(positions_ref, *refs):
+        halves = {offset: refs[2 * n : 2 * n + 2] for n, offset in enumerate(offsets)}
+        out_ref = refs[-1]
+        for tile in tiles:
+            for chip in range(out_ref.shape[1]):
+                position = positions_ref[tile, chip]
+                left_row = pl.ds(pl.multiple_of(lax.shift_right_logical(position, 2) * size, size), size)
+                right_row = pl.ds(pl.multiple_of(lax.bitwise_and(position, 3) * size, size), size)
+                left, right = TILES[tile]
+                total = None
+                for left_ref, right_ref in zip(halves[left], halves[right]):
+                    product = lax.dot_general(
+                        left_ref[left_row, :],
+                        right_ref[right_row, :],
+                        (((1,), (1,)), ((), ())),
+                        preferred_element_type=jnp.float32,
+                    )
+                    total = product if total is None else total + product
+                encode(total, out_ref.at[tile - tiles[0], chip])
+        if ready:
+            out_ref[len(tiles) :] = refs[-2][...]
+
+    count = len(tiles) + (done.shape[0] if ready else 0)
     vmem = pl.BlockSpec(memory_space=pltpu.VMEM)
+    operands = [half for offset in offsets for half in items[offset]] + ready
     return pl.pallas_call(
-        gram_kernel,
-        out_shape=jax.ShapeDtypeStruct(positions.shape + (size + TAIL, size), jnp.int16),
-        in_specs=[pl.BlockSpec(memory_space=pltpu.SMEM)] + [vmem] * len(items),
+        kernel,
+        out_shape=jax.ShapeDtypeStruct((count, positions.shape[1], size + TAIL, size), jnp.int16),
+        in_specs=[pl.BlockSpec(memory_space=pltpu.SMEM)] + [vmem] * len(operands),
         out_specs=vmem,
         compiler_params=pltpu.CompilerParams(vmem_limit_bytes=48 * 2**20),
-    )(positions, *items)
+    )(positions, *operands)
 
 
 def moved(value, axis, target):
@@ -161,12 +164,22 @@
                 wanted = jnp.where(col == tile, item[-1, :128], wanted)
     spread = jnp.broadcast_to(wanted.astype(jnp.float32), (col_count * chip_count, 128))
     gathered_positions = lax.all_to_all(spread, ("col", "chip"), 0, 0, tiled=True)
-    below2, gathered_positions = lax.optimization_barrier((below2, gathered_positions))
     positions = gathered_positions[:, 0].astype(jnp.int32).reshape(col_count, chip_count)
-    below2_other = swap_core(below2)
-    partial_sums = gram_blocks(
-        positions, (own, own_other, below, above, near_other, below2, above2, below2_other, above2_other), x_vals.shape[3]
-    )
+    size = x_vals.shape[3]
+    near_items = {
+        0: (own, own_other),
+        -1: (below, near_other[0]),
+        1: (above, near_other[1]),
+        2: (above2, above2_other),
+    }
+    partial_sums = gram_blocks(positions, NEAR, near_items, size)
+    far_items = {
+        0: (own, own_other),
+        1: (above, near_other[1]),
+        -2: (below2, swap_core(below2)),
+        2: (above2, above2_other),
+    }
+    partial_sums = gram_blocks(positions, FAR, far_items, size, partial_sums)
     partial_sums = partial_sums.reshape((-1,) + partial_sums.shape[2:])
     gathered = lax.all_to_all(partial_sums, ("col", "chip"), 0, 0, tiled=True)
     total = decode_sum(gathered)

time: 90.3 us -> 90.3 us (level)
  waiting for transfers between devices: 18.6 us -> 15.3 us
  blocking collectives: 23.2 us -> 25.5 us
    all_to_all x1, blocking collectives: 23.2 us -> 25.5 us  [on_device(): gathered = lax.all_to_all(partial_sums, ('col', 'chip'), 0, 0, tiled=True)]
    all_to_all x1, waiting for transfers between devices: 4.07 us -> 2.15 us  [on_device(): lax.all_to_all(spread, ('col', 'chip'), 0, 0, tiled=True)]
    ppermute x9, waiting for transfers between devices: 14.5 us -> 13.1 us  [moved(): lax.ppermute(value, axis, [(source, target(source)) for source in range(c...]
    pallas_call x1 -> x2, Pallas kernels: 1.39 us -> 2.22 us  [gram_blocks(): pl.pallas_call(kernel, out_shape=jax.ShapeDtypeStruct((count, positions.s...]
  transfers between devices with their start and end apart: 10 -> 10, of which waited for: 6 -> 5; matrix products, arithmetic and copies ran while one was open for 1% -> 1% of each run, Pallas kernels for 0% -> 1%
where the time goes in v3:
time: 90.3 us; the launch traced here: 89.8 us
  starting transfers between devices  40.9 us (45%)
  blocking collectives  25.5 us (28%)
  waiting for transfers between devices  15.3 us (17%)
  Pallas kernels  5.87 us (7%)
  local copies, waits for them, and re-layouts  1.34 us (1%)
    ppermute x9, starting transfers between devices, moved(): lax.ppermute(value, axis, [(source, target(source)) for source in range(c...  30.4 us
    all_to_all x1, blocking collectives, on_device(): gathered = lax.all_to_all(partial_sums, ('col', 'chip'), 0, 0, tiled=True)  25.5 us
    ppermute x9, waiting for transfers between devices, moved(): lax.ppermute(value, axis, [(source, target(source)) for source in range(c...  13.1 us
    all_to_all x1, starting transfers between devices, on_device(): lax.all_to_all(spread, ('col', 'chip'), 0, 0, tiled=True)  10.5 us
    pallas_call x2, Pallas kernels, gram_blocks(): pl.pallas_call(kernel, out_shape=jax.ShapeDtypeStruct((count, positions.s...  2.22 us
    all_to_all x1, waiting for transfers between devices, on_device(): lax.all_to_all(spread, ('col', 'chip'), 0, 0, tiled=True)  2.15 us
    pallas_call x1, Pallas kernels, densify(): pl.pallas_call(dense_kernel, out_shape=jax.ShapeDtypeStruct((slots * size...  1.82 us
    pallas_call x1, Pallas kernels, decode_sum(): pl.pallas_call(decode_sum_kernel, out_shape=jax.ShapeDtypeStruct((size, s...  1.82 us
  transfers between devices with their start and end apart: 10, of which 5 were waited for; matrix products, arithmetic and copies ran while one was open for 1% of the time, Pallas kernels for 1%

profile of v3, /device:TPU:8, one launch (start us, length us, event | category | flops | bytes accessed | tf_op | source)
XLA Modules:
  0.0 89.8 jit_solution(10852753272350689786)
XLA Ops:
  0.7 1.8 %shard_map.37.refs_2_ = bf16[528,256]{1,0:T(8,128)(2,1)} custom-call(s32[2,4]{1,0:T(2,128)} %bitcast.24, s32[1]{0:T(128)} %bitcast.17.wanted_ref, bf16[2,4,128,128]{3,2,1,0:T(8,128)(2,1)} %bitcast.21), custom_call_target="tpu_custom_call" | custom-call | tf_op jit(solution)/shard_map/pallas_call | solution.py:42
  2.5 7.7 %collective-permute-start.1 = (bf16[528,256]{1,0:T(8,128)(2,1)}, bf16[528,256]{1,0:T(8,128)(2,1)S(1)}, u32[]{:S(2)}, u32[]{:S(2)}) collective-permute-start(bf16[528,256]{1,0:T(8,128)(2,1)} %shard_map.37.refs_2_), channel_id=1, source_target_pairs={{0,480},{32,0},{64,32},{96,64},{128,96},{160,128},{192,160},{224,1... | collective-permute-start | bytes 811016 | tf_op jit(solution)/shard_map/ppermute | solution.py:129
  10.2 1.9 %collective-permute-start = (bf16[528,256]{1,0:T(8,128)(2,1)}, bf16[528,256]{1,0:T(8,128)(2,1)S(1)}, u32[]{:S(2)}, u32[]{:S(2)}) collective-permute-start(bf16[528,256]{1,0:T(8,128)(2,1)} %shard_map.37.refs_2_), channel_id=1, source_target_pairs={{0,32},{32,64},{64,96},{96,128},{128,160},{160,192},{192,224},{224... | collective-permute-start | bytes 811016 | tf_op jit(solution)/shard_map/ppermute | solution.py:129
  12.1 2.3 %collective-permute-done.1.refs_4_ = bf16[528,256]{1,0:T(8,128)(2,1)S(1)} collective-permute-done((bf16[528,256]{1,0:T(8,128)(2,1)}, bf16[528,256]{1,0:T(8,128)(2,1)S(1)}, u32[]{:S(2)}, u32[]{:S(2)}) %collective-permute-start.1) | collective-permute-done | bytes 270368 | tf_op jit(solution)/shard_map/ppermute | solution.py:129
  14.5 4.3 %collective-permute-start.2 = (bf16[528,256]{1,0:T(8,128)(2,1)S(1)}, bf16[528,256]{1,0:T(8,128)(2,1)S(1)}, u32[]{:S(2)}, u32[]{:S(2)}) collective-permute-start(bf16[528,256]{1,0:T(8,128)(2,1)S(1)} %collective-permute-done.1.refs_4_), channel_id=1, source_target_pairs={{0,480},{32,0},{64,32},{96,64},{128,96},{160,128},{192,160},{224,1... | collective-permute-start | bytes 811016 | tf_op jit(solution)/shard_map/ppermute | solution.py:129
  18.8 0.3 collective-permute-done.refs_0_
  19.1 0.0 copy-start
  19.1 0.1 pad_maximum_fusion
  19.1 2.1 %collective-permute-start.6 = (bf16[2,528,256]{2,1,0:T(8,128)(2,1)S(1)}, bf16[2,528,256]{2,1,0:T(8,128)(2,1)S(1)}, u32[]{:S(2)}, u32[]{:S(2)}) collective-permute-start(bf16[2,528,256]{2,1,0:T(8,128)(2,1)S(1)} %pad_maximum_fusion), channel_id=1, source_target_pairs={{0,1},{1,0},{2,3},{3,2},{4,5},{5,4},{6,7},{7,6},{8,9},{9,8},{10,11... | collective-permute-start | bytes 1622024 | tf_op jit(solution)/shard_map/ppermute | solution.py:129
  21.2 1.9 %collective-permute-start.3 = (bf16[528,256]{1,0:T(8,128)(2,1)S(1)}, bf16[528,256]{1,0:T(8,128)(2,1)S(1)}, u32[]{:S(2)}, u32[]{:S(2)}) collective-permute-start(bf16[528,256]{1,0:T(8,128)(2,1)S(1)} %collective-permute-done.refs_0_), channel_id=1, source_target_pairs={{0,32},{32,64},{64,96},{96,128},{128,160},{160,192},{192,224},{224... | collective-permute-start | bytes 811016 | tf_op jit(solution)/shard_map/ppermute | solution.py:129
  23.1 0.4 collective-permute-done.2.refs_6_
  23.5 0.0 copy-done
  23.6 0.6 broadcast_in_dim.3
  24.2 10.5 %all-to-all-start = ((f32[16,1,128]{2,1,0:T(1,128)}), f32[16,1,128]{2,1,0:T(1,128)S(1)}, u32[]{:S(2)}, u32[]{:S(2)}) async-start(f32[16,1,128]{2,1,0:T(1,128)} %broadcast_in_dim.3), calls=%async_computation | async-start | bytes 16384 | tf_op jit(solution)/shard_map/all_to_all | solution.py:166
  34.6 1.9 %collective-permute-start.5 = (bf16[528,256]{1,0:T(8,128)(2,1)S(1)}, bf16[528,256]{1,0:T(8,128)(2,1)S(1)}, u32[]{:S(2)}, u32[]{:S(2)}) collective-permute-start(bf16[528,256]{1,0:T(8,128)(2,1)S(1)} %copy-done), channel_id=1, source_target_pairs={{0,1},{1,0},{2,3},{3,2},{4,5},{5,4},{6,7},{7,6},{8,9},{9,8},{10,11... | collective-permute-start | bytes 811016 | tf_op jit(solution)/shard_map/ppermute | solution.py:129
  36.6 2.4 %collective-permute-start.7 = (bf16[528,256]{1,0:T(8,128)(2,1)S(1)}, bf16[528,256]{1,0:T(8,128)(2,1)S(1)}, u32[]{:S(2)}, u32[]{:S(2)}) collective-permute-start(bf16[528,256]{1,0:T(8,128)(2,1)S(1)} %collective-permute-done.2.refs_6_), channel_id=1, source_target_pairs={{0,1},{1,0},{2,3},{3,2},{4,5},{5,4},{6,7},{7,6},{8,9},{9,8},{10,11... | collective-permute-start | bytes 811016 | tf_op jit(solution)/shard_map/ppermute | solution.py:129
  39.0 0.0 collective-permute-done.3.refs_0_
  39.0 1.9 %collective-permute-start.4 = (bf16[528,256]{1,0:T(8,128)(2,1)S(1)}, bf16[528,256]{1,0:T(8,128)(2,1)S(1)}, u32[]{:S(2)}, u32[]{:S(2)}) collective-permute-start(bf16[528,256]{1,0:T(8,128)(2,1)S(1)} %collective-permute-done.3.refs_0_), channel_id=1, source_target_pairs={{0,1},{1,0},{2,3},{3,2},{4,5},{5,4},{6,7},{7,6},{8,9},{9,8},{10,11... | collective-permute-start | bytes 811016 | tf_op jit(solution)/shard_map/ppermute | solution.py:129
  40.9 2.1 %all-to-all-done = f32[16,1,128]{2,1,0:T(1,128)S(1)} async-done(((f32[16,1,128]{2,1,0:T(1,128)}), f32[16,1,128]{2,1,0:T(1,128)S(1)}, u32[]{:S(2)}, u32[]{:S(2)}) %all-to-all-start) | async-done | bytes 8224 | tf_op jit(solution)/shard_map/all_to_all | solution.py:166
  43.1 0.1 fusion
  43.2 0.1 convert_element_type.16.positions_ref
  43.2 0.0 collective-permute-done.6
  43.3 0.0 collective-permute-done.5.refs_3_
  43.3 0.0 collective-permute-done.7.refs_7_
  43.3 1.2 %shard_map.38.refs_8_ = s16[5,2,136,128]{3,2,1,0:T(8,128)(2,1)S(1)} custom-call(s32[8,2]{1,0:T(8,128)S(1)} %convert_element_type.16.positions_ref, bf16[528,256]{1,0:T(8,128)(2,1)S(1)} %collective-permute-done.refs_0_, bf16[528,256]{1,0:T(8,128)(2,1)S(1)} %get-tuple-element.9.refs_1_, bf16[528,256]{1,0:T(8,128)(2,1)S(1)} %copy-done, ...), custom_call_target="tpu_custom_call" | custom-call | tf_op jit(solution)/shard_map/pallas_call | solution.py:118
  44.5 0.0 collective-permute-done.4.refs_1_
  44.5 1.0 %shard_map.39 = s16[8,2,136,128]{3,2,1,0:T(8,128)(2,1)S(1)} custom-call(s32[8,2]{1,0:T(8,128)S(1)} %convert_element_type.16.positions_ref, bf16[528,256]{1,0:T(8,128)(2,1)S(1)} %collective-permute-done.3.refs_0_, bf16[528,256]{1,0:T(8,128)(2,1)S(1)} %collective-permute-done.4.refs_1_, bf16[528,256]{1,0:T(8,128)(2,1)S(1)} %copy-done, ...), custom_call_target="tpu_custom_call" | custom-call | tf_op jit(solution)/shard_map/pallas_call | solution.py:118
  45.6 25.5 %all_to_all.14.code_ref = s16[16,136,128]{2,1,0:T(8,128)(2,1)} all-to-all(s16[16,136,128]{2,1,0:T(8,128)(2,1)S(1)} %bitcast.19), channel_id=1, replica_groups=mesh['row'=16,'col'=8,'chip'=2,'core'=2] {'col','chip'}, dimensions={0} | all-to-all | bytes 1114112 | tf_op jit(solution)/shard_map/all_to_all | solution.py:184
  71.0 1.8 %shard_map.40 = bf16[128,128]{1,0:T(8,128)(2,1)} custom-call(s16[16,136,128]{2,1,0:T(8,128)(2,1)} %all_to_all.14.code_ref), custom_call_target="tpu_custom_call" | custom-call | tf_op jit(solution)/shard_map/pallas_call | solution.py:81
  72.9 6.3 %collective-permute-start.8 = (bf16[128,128]{1,0:T(8,128)(2,1)}, bf16[128,128]{1,0:T(8,128)(2,1)S(1)}, u32[]{:S(2)}, u32[]{:S(2)}) collective-permute-start(bf16[128,128]{1,0:T(8,128)(2,1)} %shard_map.40), channel_id=1, source_target_pairs={{0,64},{4,36},{8,8},{12,12},{16,16},{20,20},{24,24},{28,508},{32,9... | collective-permute-start | bytes 98312 | tf_op jit(solution)/shard_map/ppermute | solution.py:129
  79.1 10.0 %collective-permute-done.8 = bf16[128,128]{1,0:T(8,128)(2,1)S(1)} collective-permute-done((bf16[128,128]{1,0:T(8,128)(2,1)}, bf16[128,128]{1,0:T(8,128)(2,1)S(1)}, u32[]{:S(2)}, u32[]{:S(2)}) %collective-permute-start.8) | collective-permute-done | bytes 32800 | tf_op jit(solution)/shard_map/ppermute | solution.py:129
  89.2 0.6 copy.6
  (2 shorter events, 0.0 us)
Async XLA Ops:
  2.5 12.0 %collective-permute-start.1 = (bf16[528,256]{1,0:T(8,128)(2,1)}, bf16[528,256]{1,0:T(8,128)(2,1)S(1)}, u32[]{:S(2)}, u32[]{:S(2)}) collective-permute-start(bf16[528,256]{1,0:T(8,128)(2,1)} %shard_map.37.refs_2_), channel_id=1, source_target_pairs={{0,480},{32,0},{64,32},{96,64},{128,96},{160,128},{192,160},{224,1... | collective-permute-start | bytes 811016 | tf_op jit(solution)/shard_map/ppermute | solution.py:129
  10.2 8.9 %collective-permute-start = (bf16[528,256]{1,0:T(8,128)(2,1)}, bf16[528,256]{1,0:T(8,128)(2,1)S(1)}, u32[]{:S(2)}, u32[]{:S(2)}) collective-permute-start(bf16[528,256]{1,0:T(8,128)(2,1)} %shard_map.37.refs_2_), channel_id=1, source_target_pairs={{0,32},{32,64},{64,96},{96,128},{128,160},{160,192},{192,224},{224... | collective-permute-start | bytes 811016 | tf_op jit(solution)/shard_map/ppermute | solution.py:129
  14.5 9.1 %collective-permute-start.2 = (bf16[528,256]{1,0:T(8,128)(2,1)S(1)}, bf16[528,256]{1,0:T(8,128)(2,1)S(1)}, u32[]{:S(2)}, u32[]{:S(2)}) collective-permute-start(bf16[528,256]{1,0:T(8,128)(2,1)S(1)} %collective-permute-done.1.refs_4_), channel_id=1, source_target_pairs={{0,480},{32,0},{64,32},{96,64},{128,96},{160,128},{192,160},{224,1... | collective-permute-start | bytes 811016 | tf_op jit(solution)/shard_map/ppermute | solution.py:129
  19.1 4.5 %copy-start = (bf16[528,256]{1,0:T(8,128)(2,1)S(1)}, bf16[528,256]{1,0:T(8,128)(2,1)}, u32[]{:S(2)}) copy-start(bf16[528,256]{1,0:T(8,128)(2,1)} %shard_map.37.refs_2_) | copy-start | bytes 811012
  19.1 24.1 %collective-permute-start.6 = (bf16[2,528,256]{2,1,0:T(8,128)(2,1)S(1)}, bf16[2,528,256]{2,1,0:T(8,128)(2,1)S(1)}, u32[]{:S(2)}, u32[]{:S(2)}) collective-permute-start(bf16[2,528,256]{2,1,0:T(8,128)(2,1)S(1)} %pad_maximum_fusion), channel_id=1, source_target_pairs={{0,1},{1,0},{2,3},{3,2},{4,5},{5,4},{6,7},{7,6},{8,9},{9,8},{10,11... | collective-permute-start | bytes 1622024 | tf_op jit(solution)/shard_map/ppermute | solution.py:129
  21.2 17.8 %collective-permute-start.3 = (bf16[528,256]{1,0:T(8,128)(2,1)S(1)}, bf16[528,256]{1,0:T(8,128)(2,1)S(1)}, u32[]{:S(2)}, u32[]{:S(2)}) collective-permute-start(bf16[528,256]{1,0:T(8,128)(2,1)S(1)} %collective-permute-done.refs_0_), channel_id=1, source_target_pairs={{0,32},{32,64},{64,96},{96,128},{128,160},{160,192},{192,224},{224... | collective-permute-start | bytes 811016 | tf_op jit(solution)/shard_map/ppermute | solution.py:129
  24.2 18.9 %all-to-all-start = ((f32[16,1,128]{2,1,0:T(1,128)}), f32[16,1,128]{2,1,0:T(1,128)S(1)}, u32[]{:S(2)}, u32[]{:S(2)}) async-start(f32[16,1,128]{2,1,0:T(1,128)} %broadcast_in_dim.3), calls=%async_computation | async-start | bytes 16384 | tf_op jit(solution)/shard_map/all_to_all | solution.py:166
  34.6 8.7 %collective-permute-start.5 = (bf16[528,256]{1,0:T(8,128)(2,1)S(1)}, bf16[528,256]{1,0:T(8,128)(2,1)S(1)}, u32[]{:S(2)}, u32[]{:S(2)}) collective-permute-start(bf16[528,256]{1,0:T(8,128)(2,1)S(1)} %copy-done), channel_id=1, source_target_pairs={{0,1},{1,0},{2,3},{3,2},{4,5},{5,4},{6,7},{7,6},{8,9},{9,8},{10,11... | collective-permute-start | bytes 811016 | tf_op jit(solution)/shard_map/ppermute | solution.py:129
  36.6 6.8 %collective-permute-start.7 = (bf16[528,256]{1,0:T(8,128)(2,1)S(1)}, bf16[528,256]{1,0:T(8,128)(2,1)S(1)}, u32[]{:S(2)}, u32[]{:S(2)}) collective-permute-start(bf16[528,256]{1,0:T(8,128)(2,1)S(1)} %collective-permute-done.2.refs_6_), channel_id=1, source_target_pairs={{0,1},{1,0},{2,3},{3,2},{4,5},{5,4},{6,7},{7,6},{8,9},{9,8},{10,11... | collective-permute-start | bytes 811016 | tf_op jit(solution)/shard_map/ppermute | solution.py:129
  39.0 5.5 %collective-permute-start.4 = (bf16[528,256]{1,0:T(8,128)(2,1)S(1)}, bf16[528,256]{1,0:T(8,128)(2,1)S(1)}, u32[]{:S(2)}, u32[]{:S(2)}) collective-permute-start(bf16[528,256]{1,0:T(8,128)(2,1)S(1)} %collective-permute-done.3.refs_0_), channel_id=1, source_target_pairs={{0,1},{1,0},{2,3},{3,2},{4,5},{5,4},{6,7},{7,6},{8,9},{9,8},{10,11... | collective-permute-start | bytes 811016 | tf_op jit(solution)/shard_map/ppermute | solution.py:129
  72.9 16.3 %collective-permute-start.8 = (bf16[128,128]{1,0:T(8,128)(2,1)}, bf16[128,128]{1,0:T(8,128)(2,1)S(1)}, u32[]{:S(2)}, u32[]{:S(2)}) collective-permute-start(bf16[128,128]{1,0:T(8,128)(2,1)} %shard_map.40), channel_id=1, source_target_pairs={{0,64},{4,36},{8,8},{12,12},{16,16},{20,20},{24,24},{28,508},{32,9... | collective-permute-start | bytes 98312 | tf_op jit(solution)/shard_map/ppermute | solution.py:129

commit v4 on v3

--- a/solution.py
+++ b/solution.py
@@ -65,25 +65,11 @@
     code_ref[size:] = tail.astype(jnp.int16)
 
 
-def decode_sum_kernel(code_ref, out_ref):
-    size = out_ref.shape[0]
-    total = None
-    for part in range(code_ref.shape[0]):
-        tail = code_ref[part, size:].astype(jnp.int32)
-        value = code_ref[part, :size].astype(jnp.int32).astype(jnp.float32) * step_of(tail[0:1], tail[1:2])
-        total = value if total is None else total + value
-    out_ref[...] = total.astype(out_ref.dtype)
-
-
 def decode_sum(codes):
     size = codes.shape[2]
-    vmem = pl.BlockSpec(memory_space=pltpu.VMEM)
-    return pl.pallas_call(
-        decode_sum_kernel,
-        out_shape=jax.ShapeDtypeStruct((size, size), jnp.bfloat16),
-        in_specs=[vmem],
-        out_specs=vmem,
-    )(codes)
+    steps = codes[:, size : size + 2].astype(jnp.int32)
+    steps = step_of(steps[:, :1], steps[:, 1:])
+    return jnp.sum(codes[:, :size].astype(jnp.float32) * steps, axis=0).astype(jnp.bfloat16)
 
 
 def gram_blocks(positions, tiles, items, size, done=None):

time: 90.3 us -> 88.3 us (0.978)
  Pallas kernels: 5.87 us -> 4.03 us
    pallas_call x1 -> x0, Pallas kernels: 1.82 us -> none  [decode_sum(): pl.pallas_call(decode_sum_kernel, out_shape=jax.ShapeDtypeStruct((size, s...]
where the time goes in v4:
time: 88.3 us; the launch traced here: 87.9 us
  starting transfers between devices  40.9 us (46%)
  blocking collectives  25.4 us (29%)
  waiting for transfers between devices  15 us (17%)
  Pallas kernels  4.03 us (5%)
  local copies, waits for them, and re-layouts  1.35 us (2%)
    ppermute x9, starting transfers between devices, moved(): lax.ppermute(value, axis, [(source, target(source)) for source in range(c...  30.4 us
    all_to_all x1, blocking collectives, on_device(): gathered = lax.all_to_all(partial_sums, ('col', 'chip'), 0, 0, tiled=True)  25.4 us
    ppermute x9, waiting for transfers between devices, moved(): lax.ppermute(value, axis, [(source, target(source)) for source in range(c...  12.9 us
    all_to_all x1, starting transfers between devices, on_device(): lax.all_to_all(spread, ('col', 'chip'), 0, 0, tiled=True)  10.5 us
    pallas_call x2, Pallas kernels, gram_blocks(): pl.pallas_call(kernel, out_shape=jax.ShapeDtypeStruct((count, positions.s...  2.22 us
    all_to_all x1, waiting for transfers between devices, on_device(): lax.all_to_all(spread, ('col', 'chip'), 0, 0, tiled=True)  2.15 us
    pallas_call x1, Pallas kernels, densify(): pl.pallas_call(dense_kernel, out_shape=jax.ShapeDtypeStruct((slots * size...  1.81 us
  transfers between devices with their start and end apart: 10, of which 5 were waited for; matrix products, arithmetic and copies ran while one was open for 1% of the time, Pallas kernels for 1%

profile of v4, /device:TPU:8, one launch (start us, length us, event | category | flops | bytes accessed | tf_op | source)
XLA Modules:
  0.0 87.9 jit_solution(5162355939991869450)
XLA Ops:
  0.7 1.8 %shard_map.37.refs_2_ = bf16[528,256]{1,0:T(8,128)(2,1)} custom-call(s32[2,4]{1,0:T(2,128)} %bitcast.26, s32[1]{0:T(128)} %bitcast.19.wanted_ref, bf16[2,4,128,128]{3,2,1,0:T(8,128)(2,1)} %bitcast.23), custom_call_target="tpu_custom_call" | custom-call | tf_op jit(solution)/shard_map/pallas_call | solution.py:42
  2.5 7.7 %collective-permute-start.1 = (bf16[528,256]{1,0:T(8,128)(2,1)}, bf16[528,256]{1,0:T(8,128)(2,1)S(1)}, u32[]{:S(2)}, u32[]{:S(2)}) collective-permute-start(bf16[528,256]{1,0:T(8,128)(2,1)} %shard_map.37.refs_2_), channel_id=1, source_target_pairs={{0,480},{32,0},{64,32},{96,64},{128,96},{160,128},{192,160},{224,1... | collective-permute-start | bytes 811016 | tf_op jit(solution)/shard_map/ppermute | solution.py:115
  10.2 1.9 %collective-permute-start = (bf16[528,256]{1,0:T(8,128)(2,1)}, bf16[528,256]{1,0:T(8,128)(2,1)S(1)}, u32[]{:S(2)}, u32[]{:S(2)}) collective-permute-start(bf16[528,256]{1,0:T(8,128)(2,1)} %shard_map.37.refs_2_), channel_id=1, source_target_pairs={{0,32},{32,64},{64,96},{96,128},{128,160},{160,192},{192,224},{224... | collective-permute-start | bytes 811016 | tf_op jit(solution)/shard_map/ppermute | solution.py:115
  12.1 2.3 %collective-permute-done.1.refs_4_ = bf16[528,256]{1,0:T(8,128)(2,1)S(1)} collective-permute-done((bf16[528,256]{1,0:T(8,128)(2,1)}, bf16[528,256]{1,0:T(8,128)(2,1)S(1)}, u32[]{:S(2)}, u32[]{:S(2)}) %collective-permute-start.1) | collective-permute-done | bytes 270368 | tf_op jit(solution)/shard_map/ppermute | solution.py:115
  14.5 4.3 %collective-permute-start.2 = (bf16[528,256]{1,0:T(8,128)(2,1)S(1)}, bf16[528,256]{1,0:T(8,128)(2,1)S(1)}, u32[]{:S(2)}, u32[]{:S(2)}) collective-permute-start(bf16[528,256]{1,0:T(8,128)(2,1)S(1)} %collective-permute-done.1.refs_4_), channel_id=1, source_target_pairs={{0,480},{32,0},{64,32},{96,64},{128,96},{160,128},{192,160},{224,1... | collective-permute-start | bytes 811016 | tf_op jit(solution)/shard_map/ppermute | solution.py:115
  18.7 0.3 collective-permute-done.refs_0_
  19.1 0.0 copy-start
  19.1 0.1 pad_maximum_fusion
  19.1 2.1 %collective-permute-start.6 = (bf16[2,528,256]{2,1,0:T(8,128)(2,1)S(1)}, bf16[2,528,256]{2,1,0:T(8,128)(2,1)S(1)}, u32[]{:S(2)}, u32[]{:S(2)}) collective-permute-start(bf16[2,528,256]{2,1,0:T(8,128)(2,1)S(1)} %pad_maximum_fusion), channel_id=1, source_target_pairs={{0,1},{1,0},{2,3},{3,2},{4,5},{5,4},{6,7},{7,6},{8,9},{9,8},{10,11... | collective-permute-start | bytes 1622024 | tf_op jit(solution)/shard_map/ppermute | solution.py:115
  21.2 1.9 %collective-permute-start.3 = (bf16[528,256]{1,0:T(8,128)(2,1)S(1)}, bf16[528,256]{1,0:T(8,128)(2,1)S(1)}, u32[]{:S(2)}, u32[]{:S(2)}) collective-permute-start(bf16[528,256]{1,0:T(8,128)(2,1)S(1)} %collective-permute-done.refs_0_), channel_id=1, source_target_pairs={{0,32},{32,64},{64,96},{96,128},{128,160},{160,192},{192,224},{224... | collective-permute-start | bytes 811016 | tf_op jit(solution)/shard_map/ppermute | solution.py:115
  23.1 0.4 collective-permute-done.2.refs_6_
  23.5 0.0 copy-done
  23.5 0.6 broadcast_in_dim.3
  24.1 10.5 %all-to-all-start = ((f32[16,1,128]{2,1,0:T(1,128)}), f32[16,1,128]{2,1,0:T(1,128)S(1)}, u32[]{:S(2)}, u32[]{:S(2)}) async-start(f32[16,1,128]{2,1,0:T(1,128)} %broadcast_in_dim.3), calls=%async_computation | async-start | bytes 16384 | tf_op jit(solution)/shard_map/all_to_all | solution.py:152
  34.6 1.9 %collective-permute-start.5 = (bf16[528,256]{1,0:T(8,128)(2,1)S(1)}, bf16[528,256]{1,0:T(8,128)(2,1)S(1)}, u32[]{:S(2)}, u32[]{:S(2)}) collective-permute-start(bf16[528,256]{1,0:T(8,128)(2,1)S(1)} %copy-done), channel_id=1, source_target_pairs={{0,1},{1,0},{2,3},{3,2},{4,5},{5,4},{6,7},{7,6},{8,9},{9,8},{10,11... | collective-permute-start | bytes 811016 | tf_op jit(solution)/shard_map/ppermute | solution.py:115
  36.5 2.4 %collective-permute-start.7 = (bf16[528,256]{1,0:T(8,128)(2,1)S(1)}, bf16[528,256]{1,0:T(8,128)(2,1)S(1)}, u32[]{:S(2)}, u32[]{:S(2)}) collective-permute-start(bf16[528,256]{1,0:T(8,128)(2,1)S(1)} %collective-permute-done.2.refs_6_), channel_id=1, source_target_pairs={{0,1},{1,0},{2,3},{3,2},{4,5},{5,4},{6,7},{7,6},{8,9},{9,8},{10,11... | collective-permute-start | bytes 811016 | tf_op jit(solution)/shard_map/ppermute | solution.py:115
  38.9 0.0 collective-permute-done.3.refs_0_
  39.0 1.9 %collective-permute-start.4 = (bf16[528,256]{1,0:T(8,128)(2,1)S(1)}, bf16[528,256]{1,0:T(8,128)(2,1)S(1)}, u32[]{:S(2)}, u32[]{:S(2)}) collective-permute-start(bf16[528,256]{1,0:T(8,128)(2,1)S(1)} %collective-permute-done.3.refs_0_), channel_id=1, source_target_pairs={{0,1},{1,0},{2,3},{3,2},{4,5},{5,4},{6,7},{7,6},{8,9},{9,8},{10,11... | collective-permute-start | bytes 811016 | tf_op jit(solution)/shard_map/ppermute | solution.py:115
  40.9 2.1 %all-to-all-done = f32[16,1,128]{2,1,0:T(1,128)S(1)} async-done(((f32[16,1,128]{2,1,0:T(1,128)}), f32[16,1,128]{2,1,0:T(1,128)S(1)}, u32[]{:S(2)}, u32[]{:S(2)}) %all-to-all-start) | async-done | bytes 8224 | tf_op jit(solution)/shard_map/all_to_all | solution.py:152
  43.0 0.1 fusion.6
  43.1 0.1 convert_element_type.31.positions_ref
  43.2 0.0 collective-permute-done.6
  43.3 0.0 collective-permute-done.5.refs_3_
  43.3 0.0 collective-permute-done.7.refs_7_
  43.3 1.2 %shard_map.38.refs_8_ = s16[5,2,136,128]{3,2,1,0:T(8,128)(2,1)S(1)} custom-call(s32[8,2]{1,0:T(8,128)S(1)} %convert_element_type.31.positions_ref, bf16[528,256]{1,0:T(8,128)(2,1)S(1)} %collective-permute-done.refs_0_, bf16[528,256]{1,0:T(8,128)(2,1)S(1)} %get-tuple-element.9.refs_1_, bf16[528,256]{1,0:T(8,128)(2,1)S(1)} %copy-done, ...), custom_call_target="tpu_custom_call" | custom-call | tf_op jit(solution)/shard_map/pallas_call | solution.py:104
  44.5 0.0 collective-permute-done.4.refs_1_
  44.5 1.0 %shard_map.39 = s16[8,2,136,128]{3,2,1,0:T(8,128)(2,1)S(1)} custom-call(s32[8,2]{1,0:T(8,128)S(1)} %convert_element_type.31.positions_ref, bf16[528,256]{1,0:T(8,128)(2,1)S(1)} %collective-permute-done.3.refs_0_, bf16[528,256]{1,0:T(8,128)(2,1)S(1)} %collective-permute-done.4.refs_1_, bf16[528,256]{1,0:T(8,128)(2,1)S(1)} %copy-done, ...), custom_call_target="tpu_custom_call" | custom-call | tf_op jit(solution)/shard_map/pallas_call | solution.py:104
  45.5 25.4 %all_to_all.14 = s16[16,136,128]{2,1,0:T(8,128)(2,1)S(1)} all-to-all(s16[16,136,128]{2,1,0:T(8,128)(2,1)S(1)} %bitcast.21), channel_id=1, replica_groups=mesh['row'=16,'col'=8,'chip'=2,'core'=2] {'col','chip'}, dimensions={0} | all-to-all | bytes 1114112 | tf_op jit(solution)/shard_map/all_to_all | solution.py:170
  71.0 0.2 multiply_reduce_fusion
  71.2 6.3 %collective-permute-start.8 = (bf16[128,128]{1,0:T(8,128)(2,1)S(1)}, bf16[128,128]{1,0:T(8,128)(2,1)S(1)}, u32[]{:S(2)}, u32[]{:S(2)}) collective-permute-start(bf16[128,128]{1,0:T(8,128)(2,1)S(1)} %multiply_reduce_fusion), channel_id=1, source_target_pairs={{0,64},{4,36},{8,8},{12,12},{16,16},{20,20},{24,24},{28,508},{32,9... | collective-permute-start | bytes 98312 | tf_op jit(solution)/shard_map/ppermute | solution.py:115
  77.5 9.8 %collective-permute-done.8 = bf16[128,128]{1,0:T(8,128)(2,1)S(1)} collective-permute-done((bf16[128,128]{1,0:T(8,128)(2,1)S(1)}, bf16[128,128]{1,0:T(8,128)(2,1)S(1)}, u32[]{:S(2)}, u32[]{:S(2)}) %collective-permute-start.8) | collective-permute-done | bytes 32800 | tf_op jit(solution)/shard_map/ppermute | solution.py:115
  87.3 0.6 copy.10
  (5 shorter events, 0.1 us)
Async XLA Ops:
  2.5 12.0 %collective-permute-start.1 = (bf16[528,256]{1,0:T(8,128)(2,1)}, bf16[528,256]{1,0:T(8,128)(2,1)S(1)}, u32[]{:S(2)}, u32[]{:S(2)}) collective-permute-start(bf16[528,256]{1,0:T(8,128)(2,1)} %shard_map.37.refs_2_), channel_id=1, source_target_pairs={{0,480},{32,0},{64,32},{96,64},{128,96},{160,128},{192,160},{224,1... | collective-permute-start | bytes 811016 | tf_op jit(solution)/shard_map/ppermute | solution.py:115
  10.2 8.9 %collective-permute-start = (bf16[528,256]{1,0:T(8,128)(2,1)}, bf16[528,256]{1,0:T(8,128)(2,1)S(1)}, u32[]{:S(2)}, u32[]{:S(2)}) collective-permute-start(bf16[528,256]{1,0:T(8,128)(2,1)} %shard_map.37.refs_2_), channel_id=1, source_target_pairs={{0,32},{32,64},{64,96},{96,128},{128,160},{160,192},{192,224},{224... | collective-permute-start | bytes 811016 | tf_op jit(solution)/shard_map/ppermute | solution.py:115
  14.5 9.1 %collective-permute-start.2 = (bf16[528,256]{1,0:T(8,128)(2,1)S(1)}, bf16[528,256]{1,0:T(8,128)(2,1)S(1)}, u32[]{:S(2)}, u32[]{:S(2)}) collective-permute-start(bf16[528,256]{1,0:T(8,128)(2,1)S(1)} %collective-permute-done.1.refs_4_), channel_id=1, source_target_pairs={{0,480},{32,0},{64,32},{96,64},{128,96},{160,128},{192,160},{224,1... | collective-permute-start | bytes 811016 | tf_op jit(solution)/shard_map/ppermute | solution.py:115
  19.1 4.5 %copy-start = (bf16[528,256]{1,0:T(8,128)(2,1)S(1)}, bf16[528,256]{1,0:T(8,128)(2,1)}, u32[]{:S(2)}) copy-start(bf16[528,256]{1,0:T(8,128)(2,1)} %shard_map.37.refs_2_) | copy-start | bytes 811012
  19.1 24.1 %collective-permute-start.6 = (bf16[2,528,256]{2,1,0:T(8,128)(2,1)S(1)}, bf16[2,528,256]{2,1,0:T(8,128)(2,1)S(1)}, u32[]{:S(2)}, u32[]{:S(2)}) collective-permute-start(bf16[2,528,256]{2,1,0:T(8,128)(2,1)S(1)} %pad_maximum_fusion), channel_id=1, source_target_pairs={{0,1},{1,0},{2,3},{3,2},{4,5},{5,4},{6,7},{7,6},{8,9},{9,8},{10,11... | collective-permute-start | bytes 1622024 | tf_op jit(solution)/shard_map/ppermute | solution.py:115
  21.2 17.8 %collective-permute-start.3 = (bf16[528,256]{1,0:T(8,128)(2,1)S(1)}, bf16[528,256]{1,0:T(8,128)(2,1)S(1)}, u32[]{:S(2)}, u32[]{:S(2)}) collective-permute-start(bf16[528,256]{1,0:T(8,128)(2,1)S(1)} %collective-permute-done.refs_0_), channel_id=1, source_target_pairs={{0,32},{32,64},{64,96},{96,128},{128,160},{160,192},{192,224},{224... | collective-permute-start | bytes 811016 | tf_op jit(solution)/shard_map/ppermute | solution.py:115
  24.1 18.9 %all-to-all-start = ((f32[16,1,128]{2,1,0:T(1,128)}), f32[16,1,128]{2,1,0:T(1,128)S(1)}, u32[]{:S(2)}, u32[]{:S(2)}) async-start(f32[16,1,128]{2,1,0:T(1,128)} %broadcast_in_dim.3), calls=%async_computation | async-start | bytes 16384 | tf_op jit(solution)/shard_map/all_to_all | solution.py:152
  34.6 8.7 %collective-permute-start.5 = (bf16[528,256]{1,0:T(8,128)(2,1)S(1)}, bf16[528,256]{1,0:T(8,128)(2,1)S(1)}, u32[]{:S(2)}, u32[]{:S(2)}) collective-permute-start(bf16[528,256]{1,0:T(8,128)(2,1)S(1)} %copy-done), channel_id=1, source_target_pairs={{0,1},{1,0},{2,3},{3,2},{4,5},{5,4},{6,7},{7,6},{8,9},{9,8},{10,11... | collective-permute-start | bytes 811016 | tf_op jit(solution)/shard_map/ppermute | solution.py:115
  36.5 6.8 %collective-permute-start.7 = (bf16[528,256]{1,0:T(8,128)(2,1)S(1)}, bf16[528,256]{1,0:T(8,128)(2,1)S(1)}, u32[]{:S(2)}, u32[]{:S(2)}) collective-permute-start(bf16[528,256]{1,0:T(8,128)(2,1)S(1)} %collective-permute-done.2.refs_6_), channel_id=1, source_target_pairs={{0,1},{1,0},{2,3},{3,2},{4,5},{5,4},{6,7},{7,6},{8,9},{9,8},{10,11... | collective-permute-start | bytes 811016 | tf_op jit(solution)/shard_map/ppermute | solution.py:115
  39.0 5.5 %collective-permute-start.4 = (bf16[528,256]{1,0:T(8,128)(2,1)S(1)}, bf16[528,256]{1,0:T(8,128)(2,1)S(1)}, u32[]{:S(2)}, u32[]{:S(2)}) collective-permute-start(bf16[528,256]{1,0:T(8,128)(2,1)S(1)} %collective-permute-done.3.refs_0_), channel_id=1, source_target_pairs={{0,1},{1,0},{2,3},{3,2},{4,5},{5,4},{6,7},{7,6},{8,9},{9,8},{10,11... | collective-permute-start | bytes 811016 | tf_op jit(solution)/shard_map/ppermute | solution.py:115
  71.2 16.1 %collective-permute-start.8 = (bf16[128,128]{1,0:T(8,128)(2,1)S(1)}, bf16[128,128]{1,0:T(8,128)(2,1)S(1)}, u32[]{:S(2)}, u32[]{:S(2)}) collective-permute-start(bf16[128,128]{1,0:T(8,128)(2,1)S(1)} %multiply_reduce_fusion), channel_id=1, source_target_pairs={{0,64},{4,36},{8,8},{12,12},{16,16},{20,20},{24,24},{28,508},{32,9... | collective-permute-start | bytes 98312 | tf_op jit(solution)/shard_map/ppermute | solution.py:115

commit v5 on v4

--- a/solution.py
+++ b/solution.py
@@ -138,10 +138,8 @@
     above = down(own)
     below2 = up(below)
     above2 = down(above)
-    late_own, near = lax.optimization_barrier((own, jnp.stack([below, above])))
-    near_other = swap_core(near)
-    own_other = swap_core(late_own)
-    above2_other = swap_core(above2)
+    near_other = swap_core(jnp.stack([below, above]))
+    own_other, above2_other = swap_core(jnp.stack([own, above2]))
     col = lax.axis_index("col")
     wanted = own[-1, :128]
     for shift, item in ((2, above2), (1, above), (-1, below)):

time: 88.3 us -> 86.8 us (0.983)
  waiting for transfers between devices: 15 us -> 19.3 us
  blocking collectives: 25.4 us -> 21.6 us
  starting transfers between devices: 40.9 us -> 38 us
    all_to_all x1, waiting for transfers between devices: 2.15 us -> 6.35 us  [on_device(): lax.all_to_all(spread, ('col', 'chip'), 0, 0, tiled=True)]
    all_to_all x1, blocking collectives: 25.4 us -> 21.6 us  [on_device(): gathered = lax.all_to_all(partial_sums, ('col', 'chip'), 0, 0, tiled=True)]
    ppermute x9 -> x8, starting transfers between devices: 30.4 us -> 27.6 us  [moved(): lax.ppermute(value, axis, [(source, target(source)) for source in range(c...]
    ppermute x9 -> x8, waiting for transfers between devices: 12.9 us -> 12.9 us  [moved(): lax.ppermute(value, axis, [(source, target(source)) for source in range(c...]
  transfers between devices with their start and end apart: 10 -> 9, of which waited for: 5 -> 5; matrix products, arithmetic and copies ran while one was open for 1% -> 2% of each run, Pallas kernels for 1% -> 1%
where the time goes in v5:
time: 86.8 us; the launch traced here: 86.4 us
  starting transfers between devices  38 us (44%)
  blocking collectives  21.6 us (25%)
  waiting for transfers between devices  19.3 us (22%)
  Pallas kernels  4.03 us (5%)
  local copies, waits for them, and re-layouts  1.39 us (2%)
  other arithmetic  1.26 us (1%)
    ppermute x8, starting transfers between devices, moved(): lax.ppermute(value, axis, [(source, target(source)) for source in range(c...  27.6 us
    all_to_all x1, blocking collectives, on_device(): gathered = lax.all_to_all(partial_sums, ('col', 'chip'), 0, 0, tiled=True)  21.6 us
    ppermute x8, waiting for transfers between devices, moved(): lax.ppermute(value, axis, [(source, target(source)) for source in range(c...  12.9 us
    all_to_all x1, starting transfers between devices, on_device(): lax.all_to_all(spread, ('col', 'chip'), 0, 0, tiled=True)  10.4 us
    all_to_all x1, waiting for transfers between devices, on_device(): lax.all_to_all(spread, ('col', 'chip'), 0, 0, tiled=True)  6.35 us
    pallas_call x2, Pallas kernels, gram_blocks(): pl.pallas_call(kernel, out_shape=jax.ShapeDtypeStruct((count, positions.s...  2.22 us
    pallas_call x1, Pallas kernels, densify(): pl.pallas_call(dense_kernel, out_shape=jax.ShapeDtypeStruct((slots * size...  1.81 us
  transfers between devices with their start and end apart: 9, of which 5 were waited for; matrix products, arithmetic and copies ran while one was open for 2% of the time, Pallas kernels for 1%

profile of v5, /device:TPU:8, one launch (start us, length us, event | category | flops | bytes accessed | tf_op | source)
XLA Modules:
  0.0 86.4 jit_solution(3434789820807118414)
XLA Ops:
  0.7 1.8 %shard_map.37.refs_2_ = bf16[528,256]{1,0:T(8,128)(2,1)} custom-call(s32[2,4]{1,0:T(2,128)} %bitcast.34, s32[1]{0:T(128)} %bitcast.25.wanted_ref, bf16[2,4,128,128]{3,2,1,0:T(8,128)(2,1)} %bitcast.31), custom_call_target="tpu_custom_call" | custom-call | tf_op jit(solution)/shard_map/pallas_call | solution.py:42
  2.5 7.7 %collective-permute-start.1 = (bf16[528,256]{1,0:T(8,128)(2,1)}, bf16[528,256]{1,0:T(8,128)(2,1)S(1)}, u32[]{:S(2)}, u32[]{:S(2)}) collective-permute-start(bf16[528,256]{1,0:T(8,128)(2,1)} %shard_map.37.refs_2_), channel_id=1, source_target_pairs={{0,480},{32,0},{64,32},{96,64},{128,96},{160,128},{192,160},{224,1... | collective-permute-start | bytes 811016 | tf_op jit(solution)/shard_map/ppermute | solution.py:115
  10.2 1.9 %collective-permute-start = (bf16[528,256]{1,0:T(8,128)(2,1)}, bf16[528,256]{1,0:T(8,128)(2,1)S(1)}, u32[]{:S(2)}, u32[]{:S(2)}) collective-permute-start(bf16[528,256]{1,0:T(8,128)(2,1)} %shard_map.37.refs_2_), channel_id=1, source_target_pairs={{0,32},{32,64},{64,96},{96,128},{128,160},{160,192},{192,224},{224... | collective-permute-start | bytes 811016 | tf_op jit(solution)/shard_map/ppermute | solution.py:115
  12.1 2.3 %collective-permute-done.1.refs_4_ = bf16[528,256]{1,0:T(8,128)(2,1)S(1)} collective-permute-done((bf16[528,256]{1,0:T(8,128)(2,1)}, bf16[528,256]{1,0:T(8,128)(2,1)S(1)}, u32[]{:S(2)}, u32[]{:S(2)}) %collective-permute-start.1) | collective-permute-done | bytes 270368 | tf_op jit(solution)/shard_map/ppermute | solution.py:115
  14.5 4.3 %collective-permute-start.2 = (bf16[528,256]{1,0:T(8,128)(2,1)S(1)}, bf16[528,256]{1,0:T(8,128)(2,1)S(1)}, u32[]{:S(2)}, u32[]{:S(2)}) collective-permute-start(bf16[528,256]{1,0:T(8,128)(2,1)S(1)} %collective-permute-done.1.refs_4_), channel_id=1, source_target_pairs={{0,480},{32,0},{64,32},{96,64},{128,96},{160,128},{192,160},{224,1... | collective-permute-start | bytes 811016 | tf_op jit(solution)/shard_map/ppermute | solution.py:115
  18.7 0.3 collective-permute-done.refs_0_
  19.1 0.0 copy-start
  19.1 0.1 pad_maximum_fusion.1
  19.1 2.1 %collective-permute-start.6 = (bf16[2,528,256]{2,1,0:T(8,128)(2,1)S(1)}, bf16[2,528,256]{2,1,0:T(8,128)(2,1)S(1)}, u32[]{:S(2)}, u32[]{:S(2)}) collective-permute-start(bf16[2,528,256]{2,1,0:T(8,128)(2,1)S(1)} %pad_maximum_fusion.1), channel_id=1, source_target_pairs={{0,1},{1,0},{2,3},{3,2},{4,5},{5,4},{6,7},{7,6},{8,9},{9,8},{10,11... | collective-permute-start | bytes 1622024 | tf_op jit(solution)/shard_map/ppermute | solution.py:115
  21.2 1.9 %collective-permute-start.3 = (bf16[528,256]{1,0:T(8,128)(2,1)S(1)}, bf16[528,256]{1,0:T(8,128)(2,1)S(1)}, u32[]{:S(2)}, u32[]{:S(2)}) collective-permute-start(bf16[528,256]{1,0:T(8,128)(2,1)S(1)} %collective-permute-done.refs_0_), channel_id=1, source_target_pairs={{0,32},{32,64},{64,96},{96,128},{128,160},{160,192},{192,224},{224... | collective-permute-start | bytes 811016 | tf_op jit(solution)/shard_map/ppermute | solution.py:115
  23.1 0.4 collective-permute-done.2.refs_6_
  23.5 0.0 copy-done
  23.5 0.9 pad_maximum_fusion
  24.4 2.0 %collective-permute-start.5 = (bf16[2,528,256]{2,1,0:T(8,128)(2,1)}, bf16[2,528,256]{2,1,0:T(8,128)(2,1)S(1)}, u32[]{:S(2)}, u32[]{:S(2)}) collective-permute-start(bf16[2,528,256]{2,1,0:T(8,128)(2,1)} %pad_maximum_fusion), channel_id=1, source_target_pairs={{0,1},{1,0},{2,3},{3,2},{4,5},{5,4},{6,7},{7,6},{8,9},{9,8},{10,11... | collective-permute-start | bytes 1622024 | tf_op jit(solution)/shard_map/ppermute | solution.py:115
  26.4 0.6 broadcast_in_dim.3
  27.0 10.4 %all-to-all-start = ((f32[16,1,128]{2,1,0:T(1,128)}), f32[16,1,128]{2,1,0:T(1,128)S(1)}, u32[]{:S(2)}, u32[]{:S(2)}) async-start(f32[16,1,128]{2,1,0:T(1,128)} %broadcast_in_dim.3), calls=%async_computation | async-start | bytes 16384 | tf_op jit(solution)/shard_map/all_to_all | solution.py:150
  37.5 0.0 collective-permute-done.3.refs_0_
  37.5 2.1 %collective-permute-start.4 = (bf16[528,256]{1,0:T(8,128)(2,1)S(1)}, bf16[528,256]{1,0:T(8,128)(2,1)S(1)}, u32[]{:S(2)}, u32[]{:S(2)}) collective-permute-start(bf16[528,256]{1,0:T(8,128)(2,1)S(1)} %collective-permute-done.3.refs_0_), channel_id=1, source_target_pairs={{0,1},{1,0},{2,3},{3,2},{4,5},{5,4},{6,7},{7,6},{8,9},{9,8},{10,11... | collective-permute-start | bytes 811016 | tf_op jit(solution)/shard_map/ppermute | solution.py:115
  39.5 6.4 %all-to-all-done = f32[16,1,128]{2,1,0:T(1,128)S(1)} async-done(((f32[16,1,128]{2,1,0:T(1,128)}), f32[16,1,128]{2,1,0:T(1,128)S(1)}, u32[]{:S(2)}, u32[]{:S(2)}) %all-to-all-start) | async-done | bytes 8224 | tf_op jit(solution)/shard_map/all_to_all | solution.py:150
  45.9 0.1 fusion.6
  46.0 0.1 convert_element_type.31.positions_ref
  46.1 0.0 collective-permute-done.6
  46.1 0.0 collective-permute-done.5
  46.2 1.2 %shard_map.38.refs_8_ = s16[5,2,136,128]{3,2,1,0:T(8,128)(2,1)S(1)} custom-call(s32[8,2]{1,0:T(8,128)S(1)} %convert_element_type.31.positions_ref, bf16[528,256]{1,0:T(8,128)(2,1)S(1)} %collective-permute-done.refs_0_, bf16[528,256]{1,0:T(8,128)(2,1)S(1)} %get-tuple-element.5.refs_1_, bf16[528,256]{1,0:T(8,128)(2,1)S(1)} %copy-done, ...), custom_call_target="tpu_custom_call" | custom-call | tf_op jit(solution)/shard_map/pallas_call | solution.py:104
  47.4 0.0 collective-permute-done.4.refs_1_
  47.4 1.0 %shard_map.39 = s16[8,2,136,128]{3,2,1,0:T(8,128)(2,1)S(1)} custom-call(s32[8,2]{1,0:T(8,128)S(1)} %convert_element_type.31.positions_ref, bf16[528,256]{1,0:T(8,128)(2,1)S(1)} %collective-permute-done.3.refs_0_, bf16[528,256]{1,0:T(8,128)(2,1)S(1)} %collective-permute-done.4.refs_1_, bf16[528,256]{1,0:T(8,128)(2,1)S(1)} %copy-done, ...), custom_call_target="tpu_custom_call" | custom-call | tf_op jit(solution)/shard_map/pallas_call | solution.py:104
  48.4 21.6 %all_to_all.14 = s16[16,136,128]{2,1,0:T(8,128)(2,1)S(1)} all-to-all(s16[16,136,128]{2,1,0:T(8,128)(2,1)S(1)} %bitcast.29), channel_id=1, replica_groups=mesh['row'=16,'col'=8,'chip'=2,'core'=2] {'col','chip'}, dimensions={0} | all-to-all | bytes 1114112 | tf_op jit(solution)/shard_map/all_to_all | solution.py:168
  70.1 0.2 multiply_reduce_fusion
  70.3 5.6 %collective-permute-start.7 = (bf16[128,128]{1,0:T(8,128)(2,1)S(1)}, bf16[128,128]{1,0:T(8,128)(2,1)S(1)}, u32[]{:S(2)}, u32[]{:S(2)}) collective-permute-start(bf16[128,128]{1,0:T(8,128)(2,1)S(1)} %multiply_reduce_fusion), channel_id=1, source_target_pairs={{0,64},{4,36},{8,8},{12,12},{16,16},{20,20},{24,24},{28,508},{32,9... | collective-permute-start | bytes 98312 | tf_op jit(solution)/shard_map/ppermute | solution.py:115
  76.0 9.8 %collective-permute-done.7 = bf16[128,128]{1,0:T(8,128)(2,1)S(1)} collective-permute-done((bf16[128,128]{1,0:T(8,128)(2,1)S(1)}, bf16[128,128]{1,0:T(8,128)(2,1)S(1)}, u32[]{:S(2)}, u32[]{:S(2)}) %collective-permute-start.7) | collective-permute-done | bytes 32800 | tf_op jit(solution)/shard_map/ppermute | solution.py:115
  85.8 0.6 copy.10
  (6 shorter events, 0.1 us)
Async XLA Ops:
  2.5 12.0 %collective-permute-start.1 = (bf16[528,256]{1,0:T(8,128)(2,1)}, bf16[528,256]{1,0:T(8,128)(2,1)S(1)}, u32[]{:S(2)}, u32[]{:S(2)}) collective-permute-start(bf16[528,256]{1,0:T(8,128)(2,1)} %shard_map.37.refs_2_), channel_id=1, source_target_pairs={{0,480},{32,0},{64,32},{96,64},{128,96},{160,128},{192,160},{224,1... | collective-permute-start | bytes 811016 | tf_op jit(solution)/shard_map/ppermute | solution.py:115
  10.2 8.9 %collective-permute-start = (bf16[528,256]{1,0:T(8,128)(2,1)}, bf16[528,256]{1,0:T(8,128)(2,1)S(1)}, u32[]{:S(2)}, u32[]{:S(2)}) collective-permute-start(bf16[528,256]{1,0:T(8,128)(2,1)} %shard_map.37.refs_2_), channel_id=1, source_target_pairs={{0,32},{32,64},{64,96},{96,128},{128,160},{160,192},{192,224},{224... | collective-permute-start | bytes 811016 | tf_op jit(solution)/shard_map/ppermute | solution.py:115
  14.5 9.1 %collective-permute-start.2 = (bf16[528,256]{1,0:T(8,128)(2,1)S(1)}, bf16[528,256]{1,0:T(8,128)(2,1)S(1)}, u32[]{:S(2)}, u32[]{:S(2)}) collective-permute-start(bf16[528,256]{1,0:T(8,128)(2,1)S(1)} %collective-permute-done.1.refs_4_), channel_id=1, source_target_pairs={{0,480},{32,0},{64,32},{96,64},{128,96},{160,128},{192,160},{224,1... | collective-permute-start | bytes 811016 | tf_op jit(solution)/shard_map/ppermute | solution.py:115
  19.1 4.5 %copy-start = (bf16[528,256]{1,0:T(8,128)(2,1)S(1)}, bf16[528,256]{1,0:T(8,128)(2,1)}, u32[]{:S(2)}) copy-start(bf16[528,256]{1,0:T(8,128)(2,1)} %shard_map.37.refs_2_) | copy-start | bytes 811012
  19.1 27.0 %collective-permute-start.6 = (bf16[2,528,256]{2,1,0:T(8,128)(2,1)S(1)}, bf16[2,528,256]{2,1,0:T(8,128)(2,1)S(1)}, u32[]{:S(2)}, u32[]{:S(2)}) collective-permute-start(bf16[2,528,256]{2,1,0:T(8,128)(2,1)S(1)} %pad_maximum_fusion.1), channel_id=1, source_target_pairs={{0,1},{1,0},{2,3},{3,2},{4,5},{5,4},{6,7},{7,6},{8,9},{9,8},{10,11... | collective-permute-start | bytes 1622024 | tf_op jit(solution)/shard_map/ppermute | solution.py:115
  21.2 16.3 %collective-permute-start.3 = (bf16[528,256]{1,0:T(8,128)(2,1)S(1)}, bf16[528,256]{1,0:T(8,128)(2,1)S(1)}, u32[]{:S(2)}, u32[]{:S(2)}) collective-permute-start(bf16[528,256]{1,0:T(8,128)(2,1)S(1)} %collective-permute-done.refs_0_), channel_id=1, source_target_pairs={{0,32},{32,64},{64,96},{96,128},{128,160},{160,192},{192,224},{224... | collective-permute-start | bytes 811016 | tf_op jit(solution)/shard_map/ppermute | solution.py:115
  24.4 21.8 %collective-permute-start.5 = (bf16[2,528,256]{2,1,0:T(8,128)(2,1)}, bf16[2,528,256]{2,1,0:T(8,128)(2,1)S(1)}, u32[]{:S(2)}, u32[]{:S(2)}) collective-permute-start(bf16[2,528,256]{2,1,0:T(8,128)(2,1)} %pad_maximum_fusion), channel_id=1, source_target_pairs={{0,1},{1,0},{2,3},{3,2},{4,5},{5,4},{6,7},{7,6},{8,9},{9,8},{10,11... | collective-permute-start | bytes 1622024 | tf_op jit(solution)/shard_map/ppermute | solution.py:115
  27.0 18.9 %all-to-all-start = ((f32[16,1,128]{2,1,0:T(1,128)}), f32[16,1,128]{2,1,0:T(1,128)S(1)}, u32[]{:S(2)}, u32[]{:S(2)}) async-start(f32[16,1,128]{2,1,0:T(1,128)} %broadcast_in_dim.3), calls=%async_computation | async-start | bytes 16384 | tf_op jit(solution)/shard_map/all_to_all | solution.py:150
  37.5 9.9 %collective-permute-start.4 = (bf16[528,256]{1,0:T(8,128)(2,1)S(1)}, bf16[528,256]{1,0:T(8,128)(2,1)S(1)}, u32[]{:S(2)}, u32[]{:S(2)}) collective-permute-start(bf16[528,256]{1,0:T(8,128)(2,1)S(1)} %collective-permute-done.3.refs_0_), channel_id=1, source_target_pairs={{0,1},{1,0},{2,3},{3,2},{4,5},{5,4},{6,7},{7,6},{8,9},{9,8},{10,11... | collective-permute-start | bytes 811016 | tf_op jit(solution)/shard_map/ppermute | solution.py:115
  70.3 15.5 %collective-permute-start.7 = (bf16[128,128]{1,0:T(8,128)(2,1)S(1)}, bf16[128,128]{1,0:T(8,128)(2,1)S(1)}, u32[]{:S(2)}, u32[]{:S(2)}) collective-permute-start(bf16[128,128]{1,0:T(8,128)(2,1)S(1)} %multiply_reduce_fusion), channel_id=1, source_target_pairs={{0,64},{4,36},{8,8},{12,12},{16,16},{20,20},{24,24},{28,508},{32,9... | collective-permute-start | bytes 98312 | tf_op jit(solution)/shard_map/ppermute | solution.py:115

commit v6 on v5

--- a/solution.py
+++ b/solution.py
@@ -138,8 +138,8 @@
     above = down(own)
     below2 = up(below)
     above2 = down(above)
-    near_other = swap_core(jnp.stack([below, above]))
-    own_other, above2_other = swap_core(jnp.stack([own, above2]))
+    own_other, above_other = swap_core(jnp.stack([own, above]))
+    below_other, above2_other = swap_core(jnp.stack([below, above2]))
     col = lax.axis_index("col")
     wanted = own[-1, :128]
     for shift, item in ((2, above2), (1, above), (-1, below)):
@@ -152,14 +152,14 @@
     size = x_vals.shape[3]
     near_items = {
         0: (own, own_other),
-        -1: (below, near_other[0]),
-        1: (above, near_other[1]),
+        -1: (below, below_other),
+        1: (above, above_other),
         2: (above2, above2_other),
     }
     partial_sums = gram_blocks(positions, NEAR, near_items, size)
     far_items = {
         0: (own, own_other),
-        1: (above, near_other[1]),
+        1: (above, above_other),
         -2: (below2, swap_core(below2)),
         2: (above2, above2_other),
     }

time: 86.8 us -> 86.7 us (level)
  other arithmetic: 1.26 us -> 2.21 us
    another operation x2, other arithmetic: 0.91 us -> 1.86 us  [the longest x1 1 us: on_device(): own_other, above_other = swap_core(jnp.stack([own, above]))]
    ppermute x8, waiting for transfers between devices: 12.9 us -> 12 us  [moved(): lax.ppermute(value, axis, [(source, target(source)) for source in range(c...]
  transfers between devices with their start and end apart: 9 -> 9, of which waited for: 5 -> 3; matrix products, arithmetic and copies ran while one was open for 2% -> 3% of each run, Pallas kernels for 1% -> 1%
where the time goes in v6:
time: 86.7 us; the launch traced here: 86.3 us
  starting transfers between devices  37.2 us (43%)
  blocking collectives  22.1 us (25%)
  waiting for transfers between devices  18.5 us (21%)
  Pallas kernels  4.05 us (5%)
  other arithmetic  2.21 us (3%)
  local copies, waits for them, and re-layouts  1.39 us (2%)
    ppermute x8, starting transfers between devices, moved(): lax.ppermute(value, axis, [(source, target(source)) for source in range(c...  26.8 us
    all_to_all x1, blocking collectives, on_device(): gathered = lax.all_to_all(partial_sums, ('col', 'chip'), 0, 0, tiled=True)  22.1 us
    ppermute x8, waiting for transfers between devices, moved(): lax.ppermute(value, axis, [(source, target(source)) for source in range(c...  12 us
    all_to_all x1, starting transfers between devices, on_device(): lax.all_to_all(spread, ('col', 'chip'), 0, 0, tiled=True)  10.4 us
    all_to_all x1, waiting for transfers between devices, on_device(): lax.all_to_all(spread, ('col', 'chip'), 0, 0, tiled=True)  6.49 us
    pallas_call x2, Pallas kernels, gram_blocks(): pl.pallas_call(kernel, out_shape=jax.ShapeDtypeStruct((count, positions.s...  2.22 us
    pallas_call x1, Pallas kernels, densify(): pl.pallas_call(dense_kernel, out_shape=jax.ShapeDtypeStruct((slots * size...  1.83 us
  transfers between devices with their start and end apart: 9, of which 3 were waited for; matrix products, arithmetic and copies ran while one was open for 3% of the time, Pallas kernels for 1%

profile of v6, /device:TPU:8, one launch (start us, length us, event | category | flops | bytes accessed | tf_op | source)
XLA Modules:
  0.0 86.3 jit_solution(1197791765410333341)
XLA Ops:
  0.7 1.8 %shard_map.37.refs_2_ = bf16[528,256]{1,0:T(8,128)(2,1)} custom-call(s32[2,4]{1,0:T(2,128)} %bitcast.34, s32[1]{0:T(128)} %bitcast.25.wanted_ref, bf16[2,4,128,128]{3,2,1,0:T(8,128)(2,1)} %bitcast.31), custom_call_target="tpu_custom_call" | custom-call | tf_op jit(solution)/shard_map/pallas_call | solution.py:42
  2.5 7.7 %collective-permute-start.1 = (bf16[528,256]{1,0:T(8,128)(2,1)}, bf16[528,256]{1,0:T(8,128)(2,1)S(1)}, u32[]{:S(2)}, u32[]{:S(2)}) collective-permute-start(bf16[528,256]{1,0:T(8,128)(2,1)} %shard_map.37.refs_2_), channel_id=1, source_target_pairs={{0,480},{32,0},{64,32},{96,64},{128,96},{160,128},{192,160},{224,1... | collective-permute-start | bytes 811016 | tf_op jit(solution)/shard_map/ppermute | solution.py:115
  10.2 1.9 %collective-permute-start = (bf16[528,256]{1,0:T(8,128)(2,1)}, bf16[528,256]{1,0:T(8,128)(2,1)S(1)}, u32[]{:S(2)}, u32[]{:S(2)}) collective-permute-start(bf16[528,256]{1,0:T(8,128)(2,1)} %shard_map.37.refs_2_), channel_id=1, source_target_pairs={{0,32},{32,64},{64,96},{96,128},{128,160},{160,192},{192,224},{224... | collective-permute-start | bytes 811016 | tf_op jit(solution)/shard_map/ppermute | solution.py:115
  12.1 2.3 %collective-permute-done.1.refs_4_ = bf16[528,256]{1,0:T(8,128)(2,1)S(1)} collective-permute-done((bf16[528,256]{1,0:T(8,128)(2,1)}, bf16[528,256]{1,0:T(8,128)(2,1)S(1)}, u32[]{:S(2)}, u32[]{:S(2)}) %collective-permute-start.1) | collective-permute-done | bytes 270368 | tf_op jit(solution)/shard_map/ppermute | solution.py:115
  14.5 4.3 %collective-permute-start.2 = (bf16[528,256]{1,0:T(8,128)(2,1)S(1)}, bf16[528,256]{1,0:T(8,128)(2,1)S(1)}, u32[]{:S(2)}, u32[]{:S(2)}) collective-permute-start(bf16[528,256]{1,0:T(8,128)(2,1)S(1)} %collective-permute-done.1.refs_4_), channel_id=1, source_target_pairs={{0,480},{32,0},{64,32},{96,64},{128,96},{160,128},{192,160},{224,1... | collective-permute-start | bytes 811016 | tf_op jit(solution)/shard_map/ppermute | solution.py:115
  18.7 1.0 %pad_maximum_fusion = bf16[2,528,256]{2,1,0:T(8,128)(2,1)S(1)} fusion(bf16[1,528,256]{2,1,0:T(8,128)(2,1)S(1)} %bitcast.27, bf16[1,528,256]{2,1,0:T(8,128)(2,1)} %bitcast.26), kind=kLoop, calls=%fused_computation.1 | loop fusion | flops 270336 | bytes 1081344 | tf_op jit(solution)/shard_map/stack | solution.py:141
  19.8 1.9 %collective-permute-start.5 = (bf16[2,528,256]{2,1,0:T(8,128)(2,1)S(1)}, bf16[2,528,256]{2,1,0:T(8,128)(2,1)S(1)}, u32[]{:S(2)}, u32[]{:S(2)}) collective-permute-start(bf16[2,528,256]{2,1,0:T(8,128)(2,1)S(1)} %pad_maximum_fusion), channel_id=1, source_target_pairs={{0,1},{1,0},{2,3},{3,2},{4,5},{5,4},{6,7},{7,6},{8,9},{9,8},{10,11... | collective-permute-start | bytes 1622024 | tf_op jit(solution)/shard_map/ppermute | solution.py:115
  21.7 0.0 collective-permute-done.refs_0_
  21.7 1.9 %collective-permute-start.3 = (bf16[528,256]{1,0:T(8,128)(2,1)S(1)}, bf16[528,256]{1,0:T(8,128)(2,1)S(1)}, u32[]{:S(2)}, u32[]{:S(2)}) collective-permute-start(bf16[528,256]{1,0:T(8,128)(2,1)S(1)} %collective-permute-done.refs_0_), channel_id=1, source_target_pairs={{0,32},{32,64},{64,96},{96,128},{128,160},{160,192},{192,224},{224... | collective-permute-start | bytes 811016 | tf_op jit(solution)/shard_map/ppermute | solution.py:115
  23.6 0.0 collective-permute-done.2.refs_6_
  23.6 0.0 copy-start
  23.7 0.9 pad_maximum_fusion.1
  24.5 2.4 %collective-permute-start.6 = (bf16[2,528,256]{2,1,0:T(8,128)(2,1)}, bf16[2,528,256]{2,1,0:T(8,128)(2,1)S(1)}, u32[]{:S(2)}, u32[]{:S(2)}) collective-permute-start(bf16[2,528,256]{2,1,0:T(8,128)(2,1)} %pad_maximum_fusion.1), channel_id=1, source_target_pairs={{0,1},{1,0},{2,3},{3,2},{4,5},{5,4},{6,7},{7,6},{8,9},{9,8},{10,11... | collective-permute-start | bytes 1622024 | tf_op jit(solution)/shard_map/ppermute | solution.py:115
  26.9 0.0 copy-done
  26.9 0.6 broadcast_in_dim.3
  27.5 10.4 %all-to-all-start = ((f32[16,1,128]{2,1,0:T(1,128)}), f32[16,1,128]{2,1,0:T(1,128)S(1)}, u32[]{:S(2)}, u32[]{:S(2)}) async-start(f32[16,1,128]{2,1,0:T(1,128)} %broadcast_in_dim.3), calls=%async_computation | async-start | bytes 16384 | tf_op jit(solution)/shard_map/all_to_all | solution.py:150
  38.0 0.0 collective-permute-done.3.refs_0_
  38.0 1.9 %collective-permute-start.4 = (bf16[528,256]{1,0:T(8,128)(2,1)S(1)}, bf16[528,256]{1,0:T(8,128)(2,1)S(1)}, u32[]{:S(2)}, u32[]{:S(2)}) collective-permute-start(bf16[528,256]{1,0:T(8,128)(2,1)S(1)} %collective-permute-done.3.refs_0_), channel_id=1, source_target_pairs={{0,1},{1,0},{2,3},{3,2},{4,5},{5,4},{6,7},{7,6},{8,9},{9,8},{10,11... | collective-permute-start | bytes 811016 | tf_op jit(solution)/shard_map/ppermute | solution.py:115
  39.9 6.5 %all-to-all-done = f32[16,1,128]{2,1,0:T(1,128)S(1)} async-done(((f32[16,1,128]{2,1,0:T(1,128)}), f32[16,1,128]{2,1,0:T(1,128)S(1)}, u32[]{:S(2)}, u32[]{:S(2)}) %all-to-all-start) | async-done | bytes 8224 | tf_op jit(solution)/shard_map/all_to_all | solution.py:150
  46.4 0.1 fusion.6
  46.5 0.1 convert_element_type.31.positions_ref
  46.6 0.0 collective-permute-done.5
  46.6 0.0 collective-permute-done.6
  46.7 1.2 %shard_map.38.refs_8_ = s16[5,2,136,128]{3,2,1,0:T(8,128)(2,1)S(1)} custom-call(s32[8,2]{1,0:T(8,128)S(1)} %convert_element_type.31.positions_ref, bf16[528,256]{1,0:T(8,128)(2,1)S(1)} %collective-permute-done.refs_0_, bf16[528,256]{1,0:T(8,128)(2,1)S(1)} %get-tuple-element.5.refs_1_, bf16[528,256]{1,0:T(8,128)(2,1)S(1)} %copy-done, ...), custom_call_target="tpu_custom_call" | custom-call | tf_op jit(solution)/shard_map/pallas_call | solution.py:104
  47.9 0.0 collective-permute-done.4.refs_1_
  47.9 1.0 %shard_map.39 = s16[8,2,136,128]{3,2,1,0:T(8,128)(2,1)S(1)} custom-call(s32[8,2]{1,0:T(8,128)S(1)} %convert_element_type.31.positions_ref, bf16[528,256]{1,0:T(8,128)(2,1)S(1)} %collective-permute-done.3.refs_0_, bf16[528,256]{1,0:T(8,128)(2,1)S(1)} %collective-permute-done.4.refs_1_, bf16[528,256]{1,0:T(8,128)(2,1)S(1)} %copy-done, ...), custom_call_target="tpu_custom_call" | custom-call | tf_op jit(solution)/shard_map/pallas_call | solution.py:104
  48.9 22.1 %all_to_all.14 = s16[16,136,128]{2,1,0:T(8,128)(2,1)S(1)} all-to-all(s16[16,136,128]{2,1,0:T(8,128)(2,1)S(1)} %bitcast.29), channel_id=1, replica_groups=mesh['row'=16,'col'=8,'chip'=2,'core'=2] {'col','chip'}, dimensions={0} | all-to-all | bytes 1114112 | tf_op jit(solution)/shard_map/all_to_all | solution.py:168
  71.1 0.2 multiply_reduce_fusion
  71.3 4.7 %collective-permute-start.7 = (bf16[128,128]{1,0:T(8,128)(2,1)S(1)}, bf16[128,128]{1,0:T(8,128)(2,1)S(1)}, u32[]{:S(2)}, u32[]{:S(2)}) collective-permute-start(bf16[128,128]{1,0:T(8,128)(2,1)S(1)} %multiply_reduce_fusion), channel_id=1, source_target_pairs={{0,64},{4,36},{8,8},{12,12},{16,16},{20,20},{24,24},{28,508},{32,9... | collective-permute-start | bytes 98312 | tf_op jit(solution)/shard_map/ppermute | solution.py:115
  76.0 9.7 %collective-permute-done.7 = bf16[128,128]{1,0:T(8,128)(2,1)S(1)} collective-permute-done((bf16[128,128]{1,0:T(8,128)(2,1)S(1)}, bf16[128,128]{1,0:T(8,128)(2,1)S(1)}, u32[]{:S(2)}, u32[]{:S(2)}) %collective-permute-start.7) | collective-permute-done | bytes 32800 | tf_op jit(solution)/shard_map/ppermute | solution.py:115
  85.6 0.6 copy.10
  (6 shorter events, 0.1 us)
Async XLA Ops:
  2.5 12.0 %collective-permute-start.1 = (bf16[528,256]{1,0:T(8,128)(2,1)}, bf16[528,256]{1,0:T(8,128)(2,1)S(1)}, u32[]{:S(2)}, u32[]{:S(2)}) collective-permute-start(bf16[528,256]{1,0:T(8,128)(2,1)} %shard_map.37.refs_2_), channel_id=1, source_target_pairs={{0,480},{32,0},{64,32},{96,64},{128,96},{160,128},{192,160},{224,1... | collective-permute-start | bytes 811016 | tf_op jit(solution)/shard_map/ppermute | solution.py:115
  10.2 11.5 %collective-permute-start = (bf16[528,256]{1,0:T(8,128)(2,1)}, bf16[528,256]{1,0:T(8,128)(2,1)S(1)}, u32[]{:S(2)}, u32[]{:S(2)}) collective-permute-start(bf16[528,256]{1,0:T(8,128)(2,1)} %shard_map.37.refs_2_), channel_id=1, source_target_pairs={{0,32},{32,64},{64,96},{96,128},{128,160},{160,192},{192,224},{224... | collective-permute-start | bytes 811016 | tf_op jit(solution)/shard_map/ppermute | solution.py:115
  14.5 9.2 %collective-permute-start.2 = (bf16[528,256]{1,0:T(8,128)(2,1)S(1)}, bf16[528,256]{1,0:T(8,128)(2,1)S(1)}, u32[]{:S(2)}, u32[]{:S(2)}) collective-permute-start(bf16[528,256]{1,0:T(8,128)(2,1)S(1)} %collective-permute-done.1.refs_4_), channel_id=1, source_target_pairs={{0,480},{32,0},{64,32},{96,64},{128,96},{160,128},{192,160},{224,1... | collective-permute-start | bytes 811016 | tf_op jit(solution)/shard_map/ppermute | solution.py:115
  19.8 26.8 %collective-permute-start.5 = (bf16[2,528,256]{2,1,0:T(8,128)(2,1)S(1)}, bf16[2,528,256]{2,1,0:T(8,128)(2,1)S(1)}, u32[]{:S(2)}, u32[]{:S(2)}) collective-permute-start(bf16[2,528,256]{2,1,0:T(8,128)(2,1)S(1)} %pad_maximum_fusion), channel_id=1, source_target_pairs={{0,1},{1,0},{2,3},{3,2},{4,5},{5,4},{6,7},{7,6},{8,9},{9,8},{10,11... | collective-permute-start | bytes 1622024 | tf_op jit(solution)/shard_map/ppermute | solution.py:115
  21.7 16.2 %collective-permute-start.3 = (bf16[528,256]{1,0:T(8,128)(2,1)S(1)}, bf16[528,256]{1,0:T(8,128)(2,1)S(1)}, u32[]{:S(2)}, u32[]{:S(2)}) collective-permute-start(bf16[528,256]{1,0:T(8,128)(2,1)S(1)} %collective-permute-done.refs_0_), channel_id=1, source_target_pairs={{0,32},{32,64},{64,96},{96,128},{128,160},{160,192},{192,224},{224... | collective-permute-start | bytes 811016 | tf_op jit(solution)/shard_map/ppermute | solution.py:115
  23.6 3.3 %copy-start = (bf16[528,256]{1,0:T(8,128)(2,1)S(1)}, bf16[528,256]{1,0:T(8,128)(2,1)}, u32[]{:S(2)}) copy-start(bf16[528,256]{1,0:T(8,128)(2,1)} %shard_map.37.refs_2_) | copy-start | bytes 811012
  24.5 22.1 %collective-permute-start.6 = (bf16[2,528,256]{2,1,0:T(8,128)(2,1)}, bf16[2,528,256]{2,1,0:T(8,128)(2,1)S(1)}, u32[]{:S(2)}, u32[]{:S(2)}) collective-permute-start(bf16[2,528,256]{2,1,0:T(8,128)(2,1)} %pad_maximum_fusion.1), channel_id=1, source_target_pairs={{0,1},{1,0},{2,3},{3,2},{4,5},{5,4},{6,7},{7,6},{8,9},{9,8},{10,11... | collective-permute-start | bytes 1622024 | tf_op jit(solution)/shard_map/ppermute | solution.py:115
  27.5 18.8 %all-to-all-start = ((f32[16,1,128]{2,1,0:T(1,128)}), f32[16,1,128]{2,1,0:T(1,128)S(1)}, u32[]{:S(2)}, u32[]{:S(2)}) async-start(f32[16,1,128]{2,1,0:T(1,128)} %broadcast_in_dim.3), calls=%async_computation | async-start | bytes 16384 | tf_op jit(solution)/shard_map/all_to_all | solution.py:150
  38.0 9.9 %collective-permute-start.4 = (bf16[528,256]{1,0:T(8,128)(2,1)S(1)}, bf16[528,256]{1,0:T(8,128)(2,1)S(1)}, u32[]{:S(2)}, u32[]{:S(2)}) collective-permute-start(bf16[528,256]{1,0:T(8,128)(2,1)S(1)} %collective-permute-done.3.refs_0_), channel_id=1, source_target_pairs={{0,1},{1,0},{2,3},{3,2},{4,5},{5,4},{6,7},{7,6},{8,9},{9,8},{10,11... | collective-permute-start | bytes 811016 | tf_op jit(solution)/shard_map/ppermute | solution.py:115
  71.3 14.4 %collective-permute-start.7 = (bf16[128,128]{1,0:T(8,128)(2,1)S(1)}, bf16[128,128]{1,0:T(8,128)(2,1)S(1)}, u32[]{:S(2)}, u32[]{:S(2)}) collective-permute-start(bf16[128,128]{1,0:T(8,128)(2,1)S(1)} %multiply_reduce_fusion), channel_id=1, source_target_pairs={{0,64},{4,36},{8,8},{12,12},{16,16},{20,20},{24,24},{28,508},{32,9... | collective-permute-start | bytes 98312 | tf_op jit(solution)/shard_map/ppermute | solution.py:115
